TPU v7x, 512 devices: a whole 4x8x8 slice. The times are simulated.
512 devices in a mesh: slab: 128 (over y, z, core), disk: 4 (over x).
Axes of the slice: x: 4, y: 8, z: 8, core: 2. Of those that a mesh axis runs over, the one named last changes fastest.
Arguments:
- thermal_anomaly: float32 [2, 128, 16384], P(None, 'slab', 'disk'), may hold values from 0.5 to 1.5
- humidity_amount: float32 [2, 128, 16384], P(None, 'slab', 'disk'), may hold values from 0.2 to 2
- slab_condensate_amount: float32 [2, 128, 16384], P(None, 'slab', 'disk'), may hold values from 0.1 to 2
- overcast_indicator: int32 [2, 16384], P(None, 'disk'), may hold values 0 or 1
- molecular_opacity: float32 [112, 128], replicated, may hold values from 0.003 to 0.1
- condensate_opacity: float32 [112], replicated, may hold values from 0.01 to 0.1
- planck_quadrature_factor: float32 [112], replicated, may hold values from 0.5 to 2
- scene_contributing_profiles: int32 [4, 262144], P(None, ('slab', 'disk')), may hold values from 0 to 16383, as said below
- scene_interpolation_factors: float32 [4, 262144], P(None, ('slab', 'disk')), may hold values from 0.1 to 1
Outputs:
- pixel_radiance: float32 [2, 16, 262144], P(None, None, ('slab', 'disk'))
Inputs may be any that keep to these rules, and one draw needn't show every extreme that they name: `scene_contributing_profiles`: every source column c of pixel p lies in the pixel's latitude strip: (c % 4096) // 32 == p // 2048.
All inputs are finite; a program needn't handle non-finite values. No bound on the sum of `overcast_indicator` on one device may be relied on, other than what follows from the above.
Results may differ from a plain program's by a relative error of at most 0.0017.
Values may be sent and summed in bfloat16 or wider, within the bound.
No kernel may reach another device: no remote copies, remote signals or barrier semaphores. Data moves between devices by JAX's collectives and lax.ppermute only.
A program may use at most 64 MiB of HBM per device.

v0:
```python
import jax
import jax.numpy as jnp
from jax import lax
from jax.sharding import PartitionSpec as P

BANDS = 16
GPB = 7


def band_block(
    temp_four, vapour_cols, cloud_cols, gas_band, cloud_band, planck_band, upper_level_mask
):
    optical_depth = (
        gas_band[:, :, None] * vapour_cols[None] + cloud_band[:, None, None] * cloud_cols[None]
    )
    optical_depth_above = jnp.einsum(
        "vh,qha->qva", upper_level_mask, optical_depth, precision=lax.Precision.HIGHEST
    )
    planck = planck_band[:, None, None] * temp_four[None]
    visible = jnp.exp(-optical_depth_above)
    emitted = jnp.sum(planck * visible * (1.0 - jnp.exp(-optical_depth)), axis=1)
    ground = planck[:, -1] * visible[:, -1] * jnp.exp(-optical_depth[:, -1])
    return jnp.sum(emitted + ground, axis=0) / gas_band.shape[0]


def local(
    thermal_anomaly,
    humidity_amount,
    slab_condensate_amount,
    overcast_indicator,
    molecular_opacity,
    condensate_opacity,
    planck_quadrature_factor,
    scene_contributing_profiles,
    scene_interpolation_factors,
):
    level_count = molecular_opacity.shape[1]
    level_index = jnp.arange(level_count)
    upper_level_mask = (level_index[None, :] < level_index[:, None]).astype(jnp.float32)
    gas_bands = molecular_opacity.reshape(BANDS, GPB, level_count)
    cloud_bands = condensate_opacity.reshape(BANDS, GPB)
    planck_bands = planck_quadrature_factor.reshape(BANDS, GPB)
    overcast_fraction_intensity = (
        slab_condensate_amount * overcast_indicator.astype(jnp.float32)[:, None, :]
    )

    def radiate(pieces):
        temp_four = pieces[0] ** 4

        def one_band(coeffs):
            return band_block(
                temp_four, pieces[1], pieces[2], coeffs[0], coeffs[1], coeffs[2], upper_level_mask
            )

        return lax.map(one_band, (gas_bands, cloud_bands, planck_bands)).astype(jnp.bfloat16)

    fields = (
        lax.all_to_all(thermal_anomaly, "slab", split_axis=2, concat_axis=1, tiled=True),
        lax.all_to_all(humidity_amount, "slab", split_axis=2, concat_axis=1, tiled=True),
        lax.all_to_all(
            overcast_fraction_intensity, "slab", split_axis=2, concat_axis=1, tiled=True
        ),
    )
    spectral_interval_intensity = lax.map(radiate, fields)
    block_cols = spectral_interval_intensity.shape[2]
    sector_cols = block_cols * lax.axis_size("slab")
    strip_rad = lax.all_gather(spectral_interval_intensity, "disk", axis=2, tiled=True)
    strip_index = (
        scene_contributing_profiles // sector_cols * block_cols
        + scene_contributing_profiles % block_cols
    )
    picked = strip_rad[:, :, strip_index].astype(jnp.float32)
    pixels = jnp.sum(picked * scene_interpolation_factors[None, None], axis=2)
    return pixels


def solution(mesh):
    in_specs = (
        P(None, "slab", "disk"),
        P(None, "slab", "disk"),
        P(None, "slab", "disk"),
        P(None, "disk"),
        P(),
        P(),
        P(),
        P(None, ("slab", "disk")),
        P(None, ("slab", "disk")),
    )
    out_specs = P(None, None, ("slab", "disk"))
    return jax.shard_map(local, mesh=mesh, in_specs=in_specs, out_specs=out_specs, check_vma=False)
```

profile of v0, /device:TPU:8, one launch (start us, length us, event | category | flops | bytes accessed | tf_op | source)
XLA Modules:
  0.0 256.1 jit_solution(13512137519433528945)
XLA Ops:
  0.0 2.7 %copy.30 = s32[2,4096]{0,1:T(8,128)} copy(s32[2,4096]{1,0:T(2,128)} %param.16) | data formatting | bytes 65536 | tf_op args[3]
  2.8 1.7 convert_element_type.12
  4.5 3.6 %copy.31 = f32[2,1,4096]{0,1,2:T(1,128)} copy(f32[2,1,4096]{2,1,0:T(1,128)S(1)} %copy-done.1) | data formatting | bytes 65536 | tf_op args[2]
  8.1 4.8 %mul.88 = f32[2,1,4096]{0,1,2:T(1,128)} multiply(f32[2,1,4096]{0,1,2:T(1,128)} %copy.31, f32[2,1,4096]{0,1,2:T(1,128)S(1)} %bitcast.47) | non-fusion elementwise | flops 8192 | bytes 98304 | tf_op jit(solution)/shard_map/mul | solution.py:44
  12.9 17.5 %all-to-all-start.1 = ((f32[2,1,4096]{0,1,2:T(1,128)}), f32[2,1,4096]{0,1,2:T(1,128)S(1)}, u32[]{:S(2)}, u32[]{:S(2)}) async-start(f32[2,1,4096]{0,1,2:T(1,128)} %mul.88), calls=%async_computation.1 | async-start | bytes 4194304 | tf_op jit(solution)/shard_map/all_to_all | solution.py:60
  30.4 3.6 %copy.28 = f32[2,1,4096]{0,1,2:T(1,128)} copy(f32[2,1,4096]{2,1,0:T(1,128)S(1)} %copy-done.2) | data formatting | bytes 65536 | tf_op args[1]
  34.0 48.8 %all-to-all-done.1 = f32[2,1,4096]{0,1,2:T(1,128)S(1)} async-done(((f32[2,1,4096]{0,1,2:T(1,128)}), f32[2,1,4096]{0,1,2:T(1,128)S(1)}, u32[]{:S(2)}, u32[]{:S(2)}) %all-to-all-start.1) | async-done | bytes 32800 | tf_op jit(solution)/shard_map/all_to_all | solution.py:60
  82.8 8.0 %all-to-all-start = ((f32[2,1,4096]{0,1,2:T(1,128)}), f32[2,1,4096]{0,1,2:T(1,128)}, u32[]{:S(2)}, u32[]{:S(2)}) async-start(f32[2,1,4096]{0,1,2:T(1,128)} %copy.28), calls=%async_computation | async-start | bytes 4194304 | tf_op jit(solution)/shard_map/all_to_all | solution.py:59
  90.8 3.6 %copy.33 = f32[2,1,4096]{0,1,2:T(1,128)} copy(f32[2,1,4096]{2,1,0:T(1,128)S(1)} %copy-done.3) | data formatting | bytes 65536 | tf_op args[0]
  94.4 48.4 %all-to-all-done = f32[2,1,4096]{0,1,2:T(1,128)} async-done(((f32[2,1,4096]{0,1,2:T(1,128)}), f32[2,1,4096]{0,1,2:T(1,128)}, u32[]{:S(2)}, u32[]{:S(2)}) %all-to-all-start) | async-done | bytes 32800 | tf_op jit(solution)/shard_map/all_to_all | solution.py:59
  142.8 8.0 %all-to-all-start.2 = ((f32[2,1,4096]{0,1,2:T(1,128)}), f32[2,1,4096]{0,1,2:T(1,128)}, u32[]{:S(2)}, u32[]{:S(2)}) async-start(f32[2,1,4096]{0,1,2:T(1,128)} %copy.33), calls=%async_computation.2 | async-start | bytes 4194304 | tf_op jit(solution)/shard_map/all_to_all | solution.py:58
  151.1 1.3 copy.36
  152.4 2.7 %copy.35 = f32[2,128,32]{1,2,0:T(8,128)S(1)} copy(f32[2,128,32]{0,2,1:T(8,128)} %bitcast.6) | data formatting | bytes 65536
  155.0 47.8 %all-to-all-done.2 = f32[2,1,4096]{0,1,2:T(1,128)} async-done(((f32[2,1,4096]{0,1,2:T(1,128)}), f32[2,1,4096]{0,1,2:T(1,128)}, u32[]{:S(2)}, u32[]{:S(2)}) %all-to-all-start.2) | async-done | bytes 32800 | tf_op jit(solution)/shard_map/all_to_all | solution.py:58
  202.9 2.7 %copy.37 = f32[2,128,32]{1,2,0:T(8,128)S(1)} copy(f32[2,128,32]{0,2,1:T(8,128)} %bitcast.9) | data formatting | bytes 65536
  205.6 24.4 %while.23 = (s32[]{:T(128)}, bf16[2,16,32]{2,1,0:T(8,128)(2,1)S(1)}, f32[2,128,32]{1,2,0:T(8,128)S(1)}, f32[2,128,32]{1,2,0:T(8,128)S(1)}, f32[2,128,32]{1,2,0:T...) while((s32[]{:T(128)}, ...), condition=%wide.region_5.6_spmd.clone, body=%wide.region_0.5_spmd.clone.sunk | while | flops 44454816 | bytes 648770 | solution.py:64
  205.6 12.1 %while.24 = (s32[]{:T(128)}, bf16[16,32]{1,0:T(8,128)(2,1)S(1)}, f32[16,7]{1,0:T(8,128)S(1)}, f32[128,32]{0,1:T(8,128)S(1)}, f32[16,7,128]{2,1,0:T(8,128)S(1)}, ...) while((s32[]{:T(128)}, bf16[16,32]{1,0:T(8,128)(2,1)S(1)}, ...), condition=%wide.region_4.4_spmd, body=%wide.region_1.3_spmd.sunk | while | flops 44413856 | bytes 476513 | solution.py:55
  217.8 12.1 %while.24 = (s32[]{:T(128)}, bf16[16,32]{1,0:T(8,128)(2,1)S(1)}, f32[16,7]{1,0:T(8,128)S(1)}, f32[128,32]{0,1:T(8,128)S(1)}, f32[16,7,128]{2,1,0:T(8,128)S(1)}, ...) while((s32[]{:T(128)}, bf16[16,32]{1,0:T(8,128)(2,1)S(1)}, ...), condition=%wide.region_4.4_spmd, body=%wide.region_1.3_spmd.sunk | while | flops 44413856 | bytes 476513 | solution.py:55
  217.8 0.4 multiply_add_fusion.3
  218.6 0.4 multiply_add_fusion.3
  230.0 12.1 %all_gather.3 = bf16[2,16,128]{1,0,2:T(2,128)(2,1)S(1)} all-gather(bf16[2,16,32]{1,0,2:T(2,128)(2,1)S(1)} %copy.38), channel_id=1, replica_groups=mesh['slab'=128,'disk'=4] {'disk'}, dimensions={2}, use_global_device_ids=true | all-gather | bytes 10240 | tf_op jit(solution)/shard_map/all_gather | solution.py:67
  242.2 7.1 %gather_fusion = bf16[2048,2,16]{2,1,0:T(2,128)(2,1)S(1)} fusion(bf16[2,16,128]{1,0,2:T(2,128)(2,1)S(1)} %all_gather.3, s32[2048]{0:T(1024)S(1)} %broadcast_clamp_fusion), kind=kCustom, calls=%fused_computation | custom fusion | bytes 270336 | tf_op jit(solution)/shard_map/gather | solution.py:72
  249.2 6.1 %fusion.15 = f32[512,2,16]{2,1,0:T(2,128)S(1)} fusion(bf16[4,512,2,16]{3,2,1,0:T(2,128)(2,1)S(1)} %bitcast.50, f32[4,512]{1,0:T(4,128)S(1)} %copy-done.4), kind=kLoop, calls=%fused_computation.32 | loop fusion | flops 180224 | bytes 204800 | tf_op jit(solution)/shard_map/reduce_sum | solution.py:73
  255.3 0.8 copy.39
  (256 shorter events, 22.5 us)
Async XLA Ops:
  2.7 1.7 copy-start.1
  12.9 17.5 %copy-start.2 = (f32[2,1,4096]{2,1,0:T(1,128)S(1)}, f32[2,1,4096]{2,1,0:T(1,128)}, u32[]{:S(2)}) copy-start(f32[2,1,4096]{2,1,0:T(1,128)} %param.14) | copy-start | bytes 98308
  12.9 69.9 %all-to-all-start.1 = ((f32[2,1,4096]{0,1,2:T(1,128)}), f32[2,1,4096]{0,1,2:T(1,128)S(1)}, u32[]{:S(2)}, u32[]{:S(2)}) async-start(f32[2,1,4096]{0,1,2:T(1,128)} %mul.88), calls=%async_computation.1 | async-start | bytes 4194304 | tf_op jit(solution)/shard_map/all_to_all | solution.py:60
  34.0 56.8 %copy-start.5 = (s32[4,512]{1,0:T(4,128)S(1)}, s32[4,512]{1,0:T(4,128)}, u32[]{:S(2)}) copy-start(s32[4,512]{1,0:T(4,128)} %param.20) | copy-start | bytes 24580
  34.0 56.8 %copy-start.3 = (f32[2,1,4096]{2,1,0:T(1,128)S(1)}, f32[2,1,4096]{2,1,0:T(1,128)}, u32[]{:S(2)}) copy-start(f32[2,1,4096]{2,1,0:T(1,128)} %param.13) | copy-start | bytes 98308
  82.8 60.0 %all-to-all-start = ((f32[2,1,4096]{0,1,2:T(1,128)}), f32[2,1,4096]{0,1,2:T(1,128)}, u32[]{:S(2)}, u32[]{:S(2)}) async-start(f32[2,1,4096]{0,1,2:T(1,128)} %copy.28), calls=%async_computation | async-start | bytes 4194304 | tf_op jit(solution)/shard_map/all_to_all | solution.py:59
  94.4 56.4 %copy-start = (f32[112,128]{1,0:T(8,128)S(1)}, f32[112,128]{1,0:T(8,128)}, u32[]{:S(2)}) copy-start(f32[112,128]{1,0:T(8,128)} %param.17) | copy-start | bytes 172036
  94.4 56.5 %copy-start.6 = (f32[112]{0:T(128)S(1)}, f32[112]{0:T(128)}, u32[]{:S(2)}) copy-start(f32[112]{0:T(128)} %param.19) | copy-start | bytes 1348
  94.4 56.5 %copy-start.7 = (f32[112]{0:T(128)S(1)}, f32[112]{0:T(128)}, u32[]{:S(2)}) copy-start(f32[112]{0:T(128)} %param.18) | copy-start | bytes 1348
  142.8 60.0 %all-to-all-start.2 = ((f32[2,1,4096]{0,1,2:T(1,128)}), f32[2,1,4096]{0,1,2:T(1,128)}, u32[]{:S(2)}, u32[]{:S(2)}) async-start(f32[2,1,4096]{0,1,2:T(1,128)} %copy.33), calls=%async_computation.2 | async-start | bytes 4194304 | tf_op jit(solution)/shard_map/all_to_all | solution.py:58
  205.5 43.7 %copy-start.4 = (f32[4,512]{1,0:T(4,128)S(1)}, f32[4,512]{1,0:T(4,128)}, u32[]{:S(2)}) copy-start(f32[4,512]{1,0:T(4,128)} %param.21) | copy-start | bytes 24580
where the time goes:
time: 257 us; the launch traced here: 256 us
  waiting for transfers between devices  145 us (56%)
  starting transfers between devices  33.5 us (13%)
  local copies, waits for them, and re-layouts  30.2 us (12%)
  other arithmetic  21 us (8%)
  matrix products  12.8 us (5%)
  blocking collectives  12.1 us (5%)
    all_to_all x1, waiting for transfers between devices, local(): lax.all_to_all(overcast_fraction_intensity, 'slab', split_axis=2, concat_...  48.8 us
    all_to_all x1, waiting for transfers between devices, local(): lax.all_to_all(humidity_amount, 'slab', split_axis=2, concat_axis=1, tile...  48.4 us
    all_to_all x1, waiting for transfers between devices, local(): lax.all_to_all(thermal_anomaly, 'slab', split_axis=2, concat_axis=1, tile...  47.8 us
    unnamed x24, local copies, waits for them, and re-layouts  20.2 us
    all_to_all x1, starting transfers between devices, local(): lax.all_to_all(overcast_fraction_intensity, 'slab', split_axis=2, concat_...  17.5 us
    dot_general x32, matrix products, band_block(): jnp.einsum('vh,qha->qva', upper_level_mask, optical_depth, precision=lax....  12.8 us
    all_gather x1, blocking collectives, local(): lax.all_gather(spectral_interval_intensity, 'disk', axis=2, tiled=True)  12.1 us
    all_to_all x1, starting transfers between devices, local(): lax.all_to_all(thermal_anomaly, 'slab', split_axis=2, concat_axis=1, tile...  7.98 us
  transfers between devices with their start and end apart: 3, of which 3 were waited for; matrix products, arithmetic and copies ran while one was open for 4% of the time, Pallas kernels for 0%

commit v1 on v0

v1 whole, which is shorter than its diff:
```python
import jax
import jax.numpy as jnp
from jax import lax
from jax.experimental import pallas as pl
from jax.experimental.pallas import tpu as pltpu
from jax.sharding import PartitionSpec as P

HOURS = 2
BANDS = 16
GPB = 7
LEVELS = 128
TAPS = 4
COLS = 32
DISKS = 4
SECTOR = 4096
PIX = 512
HALF = BANDS // 2
LANES = 128
LOG2E = 1.4426950408889634

HUM_LOW, HUM_STEP = 0.2, 1.8 / 65535.0
CON_LOW, CON_STEP = 0.1, 1.9 / 65535.0
T4_SCALE = float(2**28)


def code16(x, low, step):
    q = ((x - low) * (1.0 / step) + 0.5).astype(jnp.int32)
    return jnp.clip(q, 0, 65535)


def pack_kernel(temp_ref, hum_ref, con_ref, out_ref):
    rows = SECTOR // LANES
    t2 = temp_ref[...] * temp_ref[...]
    t4 = (t2 * t2 * T4_SCALE).astype(jnp.int32)
    hum = code16(hum_ref[...], HUM_LOW, HUM_STEP)
    con = code16(con_ref[...], CON_LOW, CON_STEP)
    gas = (hum << 16) | con
    parts = (gas[:rows], gas[rows:], t4[:rows], t4[rows:])
    lane = lax.broadcasted_iota(jnp.int32, (rows, LANES), 1) // COLS
    for dest in range(LANES // COLS):
        word = None
        for spot, part in enumerate(parts):
            shift = (spot - dest) % 4 * COLS
            moved = pltpu.roll(part, shift, 1) if shift else part
            word = moved if word is None else jnp.where(lane == spot, moved, word)
        out_ref[pl.ds(dest, rows, stride=LANES // COLS), :] = word


def spread_kernel(mol_ref, con_ref, planck_ref, gas_ref, cloud_ref, weight_ref):
    lane = lax.broadcasted_iota(jnp.int32, (HALF, LANES), 1)
    row = lax.broadcasted_iota(jnp.int32, (HALF, LANES), 0)
    first = lane < LANES // 2
    con = jnp.broadcast_to(con_ref[...], (HALF, con_ref.shape[1]))
    planck = jnp.broadcast_to(planck_ref[...], (HALF, planck_ref.shape[1]))
    glane = lax.broadcasted_iota(jnp.int32, con.shape, 1)
    grow = lax.broadcasted_iota(jnp.int32, con.shape, 0)

    def column(values, j):
        low = jnp.sum(jnp.where(glane == grow * GPB + j, values, 0.0), axis=1, keepdims=True)
        high = jnp.sum(
            jnp.where(glane == (grow + HALF) * GPB + j, values, 0.0), axis=1, keepdims=True
        )
        return jnp.where(
            first, jnp.broadcast_to(low, (HALF, LANES)), jnp.broadcast_to(high, (HALF, LANES))
        )

    for j in range(GPB):
        cloud_ref[j] = column(con, j) * -LOG2E
        weight_ref[j] = column(planck, j)

    def block(i, _):
        for j in range(GPB):
            low = mol_ref[pl.ds(j, HALF, stride=GPB), :] * -LOG2E
            high = mol_ref[pl.ds(HALF * GPB + j, HALF, stride=GPB), :] * -LOG2E
            low = pltpu.roll(low, LANES - 8 * i, 1)
            high = pltpu.roll(high, LANES - 8 * i, 1)
            for k in range(8):
                gas_ref[8 * i + k, j] = jnp.where(
                    first,
                    jnp.broadcast_to(low[:, k : k + 1], (HALF, LANES)),
                    jnp.broadcast_to(high[:, k : k + 1], (HALF, LANES)),
                )
        return 0

    lax.fori_loop(0, LEVELS // 8, block, 0)


def radiate_kernel(
    word_ref, over_ref, gas_ref, cloud_ref, weight_ref, out_ref, hum_ref, con_ref, t4_ref, diff_ref
):
    strip = lax.axis_index("slab")
    group = LANES // COLS
    block = over_ref[:, pl.ds(pl.multiple_of(strip // group * LANES, LANES), LANES)]
    lane8 = lax.broadcasted_iota(jnp.int32, (8, LANES), 1) // COLS
    overcast = None
    for spot in range(group):
        hour = spot % HOURS
        row = jnp.broadcast_to(block[hour : hour + 1], (8, LANES))
        row = pltpu.roll(row, (spot - strip % group + group) % group * COLS, 1)
        overcast = row if overcast is None else jnp.where(lane8 == spot, row, overcast)
    overcast = overcast[0:1].astype(jnp.float32)

    word = word_ref[...]
    swapped = pltpu.roll(word, LANES // 2, 1)
    first = lax.broadcasted_iota(jnp.int32, word.shape, 1) < LANES // 2
    gas = jnp.where(first, word, swapped)
    t4 = jnp.where(first, swapped, word)
    hum = lax.shift_right_logical(gas, 16)
    con = gas & 65535
    hum_ref[...] = hum.astype(jnp.float32) * HUM_STEP + HUM_LOW
    con_ref[...] = (con.astype(jnp.float32) * CON_STEP + CON_LOW) * overcast
    t4_ref[pl.ds(0, LEVELS), :] = t4.astype(jnp.float32) * (1.0 / T4_SCALE)
    t4_ref[pl.ds(LEVELS, 1), :] = t4_ref[pl.ds(LEVELS - 1, 1), :]
    diff_ref[...] = t4_ref[pl.ds(1, LEVELS), :] - t4_ref[pl.ds(0, LEVELS), :]

    zero = jnp.zeros((HALF, LANES), jnp.float32)
    clouds = [cloud_ref[j] for j in range(GPB)]

    def step(i, carry):
        depth, total = list(carry[0]), list(carry[1])
        for k in range(8):
            level = 8 * i + k
            hum_row = hum_ref[pl.ds(level, HALF, stride=0), :]
            con_row = con_ref[pl.ds(level, HALF, stride=0), :]
            diff_row = diff_ref[pl.ds(level, HALF, stride=0), :]
            for j in range(GPB):
                depth[j] = depth[j] + (gas_ref[level, j] * hum_row + clouds[j] * con_row)
                total[j] = total[j] + diff_row * jnp.exp2(depth[j])
        return tuple(depth), tuple(total)

    _, total = lax.fori_loop(0, LEVELS // 8, step, ((zero,) * GPB, (zero,) * GPB))
    top = t4_ref[pl.ds(0, HALF, stride=0), :]
    band = zero
    for j in range(GPB):
        band = band + weight_ref[j] * (top + total[j])
    band = (band / GPB).astype(jnp.bfloat16).astype(jnp.float32)
    for owner in range(DISKS):
        out_ref[owner] = band


def pixel_kernel(rad_ref, source_ref, factor_ref, out_ref):
    lane = lax.broadcasted_iota(jnp.int32, (HALF, LANES), 1) // COLS
    rows = []
    for hour in range(HOURS):
        for half in range(2):
            spot = half * HOURS + hour
            row = None
            for disk in range(DISKS):
                shift = (disk - spot) % 4 * COLS
                moved = rad_ref[disk]
                moved = pltpu.roll(moved, shift, 1) if shift else moved
                row = moved if row is None else jnp.where(lane == disk, moved, row)
            rows.append(row)
    rad = jnp.concatenate(rows, axis=0).astype(jnp.bfloat16)
    strip_cols = DISKS * COLS
    col = lax.broadcasted_iota(jnp.int32, (strip_cols, PIX), 0)
    source = source_ref[...]
    local = source // SECTOR * COLS + source % COLS
    mix = jnp.zeros((strip_cols, PIX), jnp.float32)
    for tap in range(TAPS):
        mix = mix + jnp.where(col == local[tap : tap + 1], factor_ref[tap : tap + 1, :], 0.0)
    high = mix.astype(jnp.bfloat16)
    low = (mix - high.astype(jnp.float32)).astype(jnp.bfloat16)
    out_ref[...] = jnp.dot(rad, high, preferred_element_type=jnp.float32) + jnp.dot(
        rad, low, preferred_element_type=jnp.float32
    )


def local(
    thermal_anomaly,
    humidity_amount,
    slab_condensate_amount,
    overcast_indicator,
    molecular_opacity,
    condensate_opacity,
    planck_quadrature_factor,
    scene_contributing_profiles,
    scene_interpolation_factors,
):
    f32 = jnp.float32
    rows = HOURS * SECTOR // LANES
    with jax.named_scope("pack"):
        words = pl.pallas_call(
            pack_kernel, out_shape=jax.ShapeDtypeStruct((LEVELS, LANES), jnp.int32)
        )(
            thermal_anomaly.reshape(rows, LANES),
            humidity_amount.reshape(rows, LANES),
            slab_condensate_amount.reshape(rows, LANES),
        )
    words = lax.all_to_all(words, "slab", split_axis=0, concat_axis=0, tiled=True)
    with jax.named_scope("spread"):
        gas, cloud, weight = pl.pallas_call(
            spread_kernel,
            out_shape=(
                jax.ShapeDtypeStruct((LEVELS, GPB, HALF, LANES), f32),
                jax.ShapeDtypeStruct((GPB, HALF, LANES), f32),
                jax.ShapeDtypeStruct((GPB, HALF, LANES), f32),
            ),
        )(
            molecular_opacity,
            condensate_opacity.reshape(1, -1),
            planck_quadrature_factor.reshape(1, -1),
        )
    with jax.named_scope("radiate"):
        level_cols = pltpu.VMEM((LEVELS, LANES), f32)
        radiance = pl.pallas_call(
            radiate_kernel,
            out_shape=jax.ShapeDtypeStruct((DISKS, HALF, LANES), f32),
            scratch_shapes=[level_cols, level_cols, pltpu.VMEM((LEVELS + 8, LANES), f32), level_cols],
        )(words, overcast_indicator, gas, cloud, weight)
    radiance = lax.all_to_all(radiance, "disk", split_axis=0, concat_axis=0, tiled=True)
    with jax.named_scope("pixels"):
        pixels = pl.pallas_call(
            pixel_kernel, out_shape=jax.ShapeDtypeStruct((HOURS * BANDS, PIX), f32)
        )(radiance, scene_contributing_profiles, scene_interpolation_factors)
    return pixels.reshape(HOURS, BANDS, PIX)


def solution(mesh):
    in_specs = (
        P(None, "slab", "disk"),
        P(None, "slab", "disk"),
        P(None, "slab", "disk"),
        P(None, "disk"),
        P(),
        P(),
        P(),
        P(None, ("slab", "disk")),
        P(None, ("slab", "disk")),
    )
    out_specs = P(None, None, ("slab", "disk"))
    return jax.shard_map(local, mesh=mesh, in_specs=in_specs, out_specs=out_specs, check_vma=False)
```

time: 257 us -> 46.4 us (0.18)
  waiting for transfers between devices: 145 us -> 0.01 us
  local copies, waits for them, and re-layouts: 30.2 us -> 0.63 us
  other arithmetic: 21 us -> 0 us
  Pallas kernels: 0 us -> 18.3 us
  starting transfers between devices: 33.5 us -> 17.4 us
  matrix products: 12.8 us -> 0 us
    all_to_all x3 -> x1, waiting for transfers between devices: 145 us -> 0.01 us  [local(): lax.all_to_all(words, 'slab', split_axis=0, concat_axis=0, tiled=True)]
    unnamed x24 -> x2, local copies, waits for them, and re-layouts: 20.2 us -> 0.63 us
    pallas_call x0 -> x4, Pallas kernels: none -> 18.3 us  [the longest x1 11.3 us: local(): pl.pallas_call(spread_kernel, out_shape=(jax.ShapeDtypeStruct((LEVELS, GP...]
    all_to_all x3 -> x1, starting transfers between devices: 33.5 us -> 17.4 us  [local(): lax.all_to_all(words, 'slab', split_axis=0, concat_axis=0, tiled=True)]
    dot_general x32 -> x0, matrix products: 12.8 us -> none  [band_block(): jnp.einsum('vh,qha->qva', upper_level_mask, optical_depth, precision=lax....]
    mul x35 -> x0, other arithmetic: 12.2 us -> none  [the longest x32 7.39 us: band_block(): ground = planck[:, -1] * visible[:, -1] * jnp.exp(-optical_depth[:, -1])]
    all_gather x1 -> x0, blocking collectives: 12.1 us -> none  [local(): lax.all_gather(spectral_interval_intensity, 'disk', axis=2, tiled=True)]
    all_to_all x0 -> x1, blocking collectives: none -> 9.76 us  [local(): lax.all_to_all(radiance, 'disk', split_axis=0, concat_axis=0, tiled=True)]
  transfers between devices with their start and end apart: 3 -> 1, of which waited for: 3 -> 0; matrix products, arithmetic and copies ran while one was open for 4% -> 0% of each run, Pallas kernels for 0% -> 25%
where the time goes in v1:
time: 46.4 us; the launch traced here: 46.1 us
  Pallas kernels  18.3 us (39%)
  starting transfers between devices  17.4 us (37%)
  blocking collectives  9.76 us (21%)
  local copies, waits for them, and re-layouts  0.63 us (1%)
    all_to_all x1, starting transfers between devices, local(): lax.all_to_all(words, 'slab', split_axis=0, concat_axis=0, tiled=True)  17.4 us
    pallas_call x1, Pallas kernels, local(): pl.pallas_call(spread_kernel, out_shape=(jax.ShapeDtypeStruct((LEVELS, GP...  11.3 us
    all_to_all x1, blocking collectives, local(): lax.all_to_all(radiance, 'disk', split_axis=0, concat_axis=0, tiled=True)  9.76 us
    pallas_call x1, Pallas kernels, local(): pl.pallas_call(radiate_kernel, out_shape=jax.ShapeDtypeStruct((DISKS, HAL...  3.79 us
    pallas_call x1, Pallas kernels, local(): pl.pallas_call(pixel_kernel, out_shape=jax.ShapeDtypeStruct((HOURS * BAND...  1.66 us
    pallas_call x1, Pallas kernels, local(): pl.pallas_call(pack_kernel, out_shape=jax.ShapeDtypeStruct((LEVELS, LANES...  1.55 us
  transfers between devices with their start and end apart: 1, of which 0 were waited for; matrix products, arithmetic and copies ran while one was open for 0% of the time, Pallas kernels for 25%

profile of v1, /device:TPU:8, one launch (start us, length us, event | category | flops | bytes accessed | tf_op | source)
XLA Modules:
  0.0 46.1 jit_solution(9665665120539849816)
XLA Ops:
  0.0 1.6 %pack.1 = s32[128,128]{1,0:T(8,128)} custom-call(f32[64,128]{1,0:T(8,128)} %bitcast.12, f32[64,128]{1,0:T(8,128)} %bitcast.13, f32[64,128]{1,0:T(8,128)} %bitcast.14), custom_call_target="tpu_custom_call" | custom-call | tf_op jit(solution)/shard_map/pack/pallas_call | solution.py:183
  1.6 17.4 %all-to-all-start = ((s32[128,1,128]{2,1,0:T(1,128)}), s32[128,1,128]{2,1,0:T(1,128)S(1)}, u32[]{:S(2)}, u32[]{:S(2)}) async-start(s32[128,1,128]{2,1,0:T(1,128)} %bitcast.10), calls=%async_computation | async-start | bytes 131072 | tf_op jit(solution)/shard_map/all_to_all | solution.py:190
  18.9 11.3 %spread.1 = (f32[128,7,8,128]{3,2,1,0:T(8,128)}, f32[7,8,128]{2,1,0:T(8,128)}, f32[7,8,128]{2,1,0:T(8,128)}) custom-call(f32[112,128]{1,0:T(8,128)} %mol_ref.1, f32[1,112]{1,0:T(1,128)} %bitcast.15, f32[1,112]{1,0:T(1,128)} %bitcast.16), custom_call_target="tpu_custom_call" | custom-call | tf_op jit(solution)/shard_map/spread/pallas_call | solution.py:192
  30.2 0.0 all-to-all-done
  30.2 0.0 copy-start
  30.2 0.6 %copy-done = s32[128,1,128]{2,1,0:T(1,128)} copy-done((s32[128,1,128]{2,1,0:T(1,128)}, s32[128,1,128]{2,1,0:T(1,128)S(1)}, u32[]{:S(2)}) %copy-start) | copy-done | bytes 65560
  30.9 3.8 %radiate.1 = f32[4,8,128]{2,1,0:T(8,128)} custom-call(s32[128,128]{1,0:T(8,128)} %bitcast.11, s32[2,4096]{1,0:T(2,128)} %over_ref.1, f32[128,7,8,128]{3,2,1,0:T(8,128)} %get-tuple-element.8.gas_ref, f32[7,8,128]{2,1,0:T(8,128)} %get-tuple-element.9.cloud_ref, f32[7,8,128]{2,1,0:T(8,128)} %get-tuple-element.10.weight_ref), custom_call_target="tpu_custom_call" | custom-call | tf_op jit(solution)/shard_map/radiate/pallas_call | solution.py:206
  34.7 9.8 %all_to_all.16.rad_ref = f32[4,8,128]{2,1,0:T(8,128)} all-to-all(f32[4,8,128]{2,1,0:T(8,128)} %radiate.1), channel_id=1, replica_groups=mesh['slab'=128,'disk'=4] {'disk'}, dimensions={0} | all-to-all | bytes 32768 | tf_op jit(solution)/shard_map/all_to_all | solution.py:211
  44.4 1.7 %pixels.1 = f32[32,512]{1,0:T(8,128)} custom-call(f32[4,8,128]{2,1,0:T(8,128)} %all_to_all.16.rad_ref, s32[4,512]{1,0:T(4,128)} %source_ref.1, f32[4,512]{1,0:T(4,128)} %factor_ref.1), custom_call_target="tpu_custom_call" | custom-call | tf_op jit(solution)/shard_map/pixels/pallas_call | solution.py:213
Async XLA Ops:
  1.6 28.7 %all-to-all-start = ((s32[128,1,128]{2,1,0:T(1,128)}), s32[128,1,128]{2,1,0:T(1,128)S(1)}, u32[]{:S(2)}, u32[]{:S(2)}) async-start(s32[128,1,128]{2,1,0:T(1,128)} %bitcast.10), calls=%async_computation | async-start | bytes 131072 | tf_op jit(solution)/shard_map/all_to_all | solution.py:190
  30.2 0.6 %copy-start = (s32[128,1,128]{2,1,0:T(1,128)}, s32[128,1,128]{2,1,0:T(1,128)S(1)}, u32[]{:S(2)}) copy-start(s32[128,1,128]{2,1,0:T(1,128)S(1)} %all-to-all-done) | copy-start | bytes 196612

commit v2 on v1

v2 whole, which is shorter than its diff:
```python
import jax
import jax.numpy as jnp
from jax import lax
from jax.experimental import pallas as pl
from jax.experimental.pallas import tpu as pltpu
from jax.sharding import PartitionSpec as P

HOURS = 2
BANDS = 16
GPB = 7
LEVELS = 128
TAPS = 4
COLS = 32
DISKS = 4
SECTOR = 4096
PIX = 512
HALF = BANDS // 2
LANES = 128
KEPT = 96
LOG2E = 1.4426950408889634

HUM_LOW, HUM_STEP = 0.2, 1.8 / 65535.0
CON_LOW, CON_STEP = 0.1, 1.9 / 65535.0
T4_SCALE = float(2**28)


def code16(x, low, step):
    q = ((x - low) * (1.0 / step) + 0.5).astype(jnp.int32)
    return jnp.clip(q, 0, 65535)


def pack_kernel(temp_ref, hum_ref, con_ref, out_ref):
    rows = SECTOR // LANES
    t2 = temp_ref[...] * temp_ref[...]
    t4 = (t2 * t2 * T4_SCALE).astype(jnp.int32)
    hum = code16(hum_ref[...], HUM_LOW, HUM_STEP)
    con = code16(con_ref[...], CON_LOW, CON_STEP)
    gas = (hum << 16) | con
    parts = (gas[:rows], gas[rows:], t4[:rows], t4[rows:])
    lane = lax.broadcasted_iota(jnp.int32, (rows, LANES), 1) // COLS
    for dest in range(LANES // COLS):
        word = None
        for spot, part in enumerate(parts):
            moved = turn(part, (spot - dest) % 4 * COLS)
            word = moved if word is None else jnp.where(lane == spot, moved, word)
        out_ref[pl.ds(dest, rows, stride=LANES // COLS), :] = word


def turn(x, shift):
    return x if isinstance(shift, int) and shift == 0 else pltpu.roll(x, shift, 1)


def prepare_kernel(
    mol_ref, con_ref, planck_ref, over_ref, source_ref, factor_ref,
    gas_ref, low_gas_ref, cloud_ref, weight_ref, overcast_ref, mix_ref,
):
    lane = lax.broadcasted_iota(jnp.int32, (HALF, LANES), 1)
    first = lane < LANES // 2
    con = jnp.broadcast_to(con_ref[...], (HALF, con_ref.shape[1]))
    planck = jnp.broadcast_to(planck_ref[...], (HALF, planck_ref.shape[1]))
    glane = lax.broadcasted_iota(jnp.int32, con.shape, 1)
    grow = lax.broadcasted_iota(jnp.int32, con.shape, 0)

    def column(values, j):
        low = jnp.sum(jnp.where(glane == grow * GPB + j, values, 0.0), axis=1, keepdims=True)
        high = jnp.sum(
            jnp.where(glane == (grow + HALF) * GPB + j, values, 0.0), axis=1, keepdims=True
        )
        return jnp.where(
            first, jnp.broadcast_to(low, (HALF, LANES)), jnp.broadcast_to(high, (HALF, LANES))
        )

    for j in range(GPB):
        cloud_ref[j] = column(con, j) * -LOG2E
        weight_ref[j] = column(planck, j)

    span = LANES // 4
    shape = (span * HALF, LANES)
    pick = lax.broadcasted_iota(jnp.int32, shape, 1) % span == (
        lax.broadcasted_iota(jnp.int32, shape, 0) // HALF
    )
    half_of = lambda axis: lax.broadcasted_iota(jnp.int32, (LANES, LANES), axis) // (LANES // 2)
    same_half = (half_of(0) == half_of(1)).astype(jnp.float32).astype(jnp.bfloat16)

    def levels(q, first_level, to_ref):
        for j in range(GPB):
            row = None
            for half in range(2):
                tile = mol_ref[pl.ds(half * HALF * GPB + j, HALF, stride=GPB), :] * -LOG2E
                high = tile.astype(jnp.bfloat16).astype(jnp.float32)
                for k, piece in enumerate((high, tile - high)):
                    spot = 2 * half + k
                    moved = turn(piece, (spot - q + 4) % 4 * span)
                    row = moved if row is None else jnp.where(lane // span == spot, moved, row)
            rows = jnp.broadcast_to(row[None], (span, HALF, LANES)).reshape(shape)
            rows = jnp.where(pick, rows, 0.0).astype(jnp.bfloat16)
            wide = jnp.dot(rows, same_half, preferred_element_type=jnp.float32)
            start = pl.multiple_of(first_level, span)
            to_ref[pl.ds(start, span), j] = wide.reshape(span, HALF, LANES)
        return 0

    levels(KEPT // span, 0, low_gas_ref)
    lax.fori_loop(0, KEPT // span, lambda q, _: levels(q, q * span, gas_ref), 0)

    strip = lax.axis_index("slab")
    group = LANES // COLS
    block = over_ref[:, pl.ds(pl.multiple_of(strip // group * LANES, LANES), LANES)]
    overcast = None
    for spot in range(group):
        row = jnp.broadcast_to(block[spot % HOURS : spot % HOURS + 1], (HALF, LANES))
        row = pltpu.roll(row, (spot - strip % group + group) % group * COLS, 1)
        overcast = row if overcast is None else jnp.where(lane // COLS == spot, row, overcast)
    overcast_ref[...] = overcast.astype(jnp.float32)

    strip_cols = DISKS * COLS
    col = lax.broadcasted_iota(jnp.int32, (strip_cols, PIX), 0)
    source = source_ref[...]
    local = source // SECTOR * COLS + source % COLS
    mix = jnp.zeros((strip_cols, PIX), jnp.float32)
    for tap in range(TAPS):
        mix = mix + jnp.where(col == local[tap : tap + 1], factor_ref[tap : tap + 1, :], 0.0)
    high = mix.astype(jnp.bfloat16)
    mix_ref[pl.ds(0, strip_cols), :] = high
    mix_ref[pl.ds(strip_cols, strip_cols), :] = (mix - high.astype(jnp.float32)).astype(jnp.bfloat16)


def radiate_kernel(
    word_ref, gas_ref, low_gas_ref, cloud_ref, weight_ref, overcast_ref,
    out_ref,
    tail_ref, hum_ref, con_ref, t4_ref, diff_ref, sem,
):
    copy = pltpu.make_async_copy(low_gas_ref, tail_ref, sem)
    copy.start()
    word = word_ref[...]
    swapped = pltpu.roll(word, LANES // 2, 1)
    first = lax.broadcasted_iota(jnp.int32, word.shape, 1) < LANES // 2
    gas = jnp.where(first, word, swapped)
    t4 = jnp.where(first, swapped, word)
    hum = lax.shift_right_logical(gas, 16)
    con = gas & 65535
    hum_ref[...] = hum.astype(jnp.float32) * HUM_STEP + HUM_LOW
    con_ref[...] = (con.astype(jnp.float32) * CON_STEP + CON_LOW) * overcast_ref[0:1, :]
    t4_ref[pl.ds(0, LEVELS), :] = t4.astype(jnp.float32) * (1.0 / T4_SCALE)
    t4_ref[pl.ds(LEVELS, 1), :] = t4_ref[pl.ds(LEVELS - 1, 1), :]
    diff_ref[...] = t4_ref[pl.ds(1, LEVELS), :] - t4_ref[pl.ds(0, LEVELS), :]

    zero = jnp.zeros((HALF, LANES), jnp.float32)
    clouds = [cloud_ref[j] for j in range(GPB)]

    def step(i, carry, from_ref, start):
        depth, total = list(carry[0]), list(carry[1])
        for k in range(8):
            level = 8 * i + k
            hum_row = hum_ref[pl.ds(start + level, HALF, stride=0), :]
            con_row = con_ref[pl.ds(start + level, HALF, stride=0), :]
            diff_row = diff_ref[pl.ds(start + level, HALF, stride=0), :]
            for j in range(GPB):
                depth[j] = depth[j] + (from_ref[level, j] * hum_row + clouds[j] * con_row)
                total[j] = total[j] + diff_row * jnp.exp2(depth[j])
        return tuple(depth), tuple(total)

    carry = (zero,) * GPB, (zero,) * GPB
    carry = lax.fori_loop(0, KEPT // 8, lambda i, c: step(i, c, gas_ref, 0), carry)
    copy.wait()
    _, total = lax.fori_loop(
        0, (LEVELS - KEPT) // 8, lambda i, c: step(i, c, tail_ref, KEPT), carry
    )
    top = t4_ref[pl.ds(0, HALF, stride=0), :]
    band = zero
    for j in range(GPB):
        band = band + weight_ref[j] * (top + total[j])
    band = (band / GPB).astype(jnp.bfloat16).astype(jnp.float32)
    for owner in range(DISKS):
        out_ref[owner] = band


def pixel_kernel(rad_ref, mix_ref, out_ref):
    lane = lax.broadcasted_iota(jnp.int32, (HALF, LANES), 1) // COLS
    rows = []
    for hour in range(HOURS):
        for half in range(2):
            spot = half * HOURS + hour
            row = None
            for disk in range(DISKS):
                moved = turn(rad_ref[disk], (disk - spot) % 4 * COLS)
                row = moved if row is None else jnp.where(lane == disk, moved, row)
            rows.append(row)
    rad = jnp.concatenate(rows, axis=0).astype(jnp.bfloat16)
    rad = jnp.concatenate([rad, rad], axis=1)
    out_ref[...] = jnp.dot(rad, mix_ref[...], preferred_element_type=jnp.float32)


ANY = pl.BlockSpec(memory_space=pl.ANY)
SMALL = pltpu.CompilerParams(vmem_limit_bytes=8 << 20)


def in_vmem(x):
    return pltpu.with_memory_space_constraint(x, pltpu.VMEM)


def in_hbm(x):
    return pltpu.with_memory_space_constraint(x, pltpu.HBM)


def local(
    thermal_anomaly,
    humidity_amount,
    slab_condensate_amount,
    overcast_indicator,
    molecular_opacity,
    condensate_opacity,
    planck_quadrature_factor,
    scene_contributing_profiles,
    scene_interpolation_factors,
):
    f32 = jnp.float32
    rows = HOURS * SECTOR // LANES
    level_cols = pltpu.VMEM((LEVELS, LANES), f32)
    per_point = pltpu.VMEM((GPB, HALF, LANES), f32)
    with jax.named_scope("pack"):
        words = pl.pallas_call(
            pack_kernel, out_shape=pltpu.VMEM((LEVELS, LANES), jnp.int32), compiler_params=SMALL
        )(
            in_hbm(thermal_anomaly.reshape(rows, LANES)),
            in_hbm(humidity_amount.reshape(rows, LANES)),
            in_hbm(slab_condensate_amount.reshape(rows, LANES)),
        )
    words = lax.all_to_all(words, "slab", split_axis=0, concat_axis=0, tiled=True)
    with jax.named_scope("prepare"):
        gas, low_gas, cloud, weight, overcast, mix = pl.pallas_call(
            prepare_kernel,
            out_shape=(
                pltpu.VMEM((KEPT, GPB, HALF, LANES), f32),
                pltpu.HBM((LEVELS - KEPT, GPB, HALF, LANES), f32),
                per_point,
                per_point,
                pltpu.VMEM((HALF, LANES), f32),
                pltpu.VMEM((2 * DISKS * COLS, PIX), jnp.bfloat16),
            ),
            compiler_params=SMALL,
        )(
            in_hbm(molecular_opacity),
            in_hbm(condensate_opacity.reshape(1, -1)),
            in_hbm(planck_quadrature_factor.reshape(1, -1)),
            in_hbm(overcast_indicator),
            in_hbm(scene_contributing_profiles),
            in_hbm(scene_interpolation_factors),
        )
    with jax.named_scope("radiate"):
        radiance = pl.pallas_call(
            radiate_kernel,
            out_shape=pltpu.VMEM((DISKS, HALF, LANES), f32),
            in_specs=[ANY if k == 2 else pl.BlockSpec() for k in range(6)],
            scratch_shapes=[
                pltpu.VMEM((LEVELS - KEPT, GPB, HALF, LANES), f32),
                level_cols,
                level_cols,
                pltpu.VMEM((LEVELS + 8, LANES), f32),
                level_cols,
                pltpu.SemaphoreType.DMA,
            ],
            compiler_params=SMALL,
        )(in_vmem(words), gas, in_hbm(low_gas), cloud, weight, overcast)
    radiance = lax.all_to_all(radiance, "disk", split_axis=0, concat_axis=0, tiled=True)
    with jax.named_scope("pixels"):
        pixels = pl.pallas_call(
            pixel_kernel,
            out_shape=jax.ShapeDtypeStruct((HOURS * BANDS, PIX), f32),
            compiler_params=SMALL,
        )(in_vmem(radiance), mix)
    return pixels.reshape(HOURS, BANDS, PIX)


def solution(mesh):
    in_specs = (
        P(None, "slab", "disk"),
        P(None, "slab", "disk"),
        P(None, "slab", "disk"),
        P(None, "disk"),
        P(),
        P(),
        P(),
        P(None, ("slab", "disk")),
        P(None, ("slab", "disk")),
    )
    out_specs = P(None, None, ("slab", "disk"))
    return jax.shard_map(local, mesh=mesh, in_specs=in_specs, out_specs=out_specs, check_vma=False)
```

time: 46.4 us -> 42.1 us (0.907)
  the two profiles are of different devices: /device:TPU:8 before, /device:TPU:1 now
where the time goes in v2:
time: 42.1 us; the launch traced here: 41.7 us
  starting transfers between devices  18.4 us (44%)
  waiting for transfers between devices  8.29 us (20%)
  blocking collectives  8.03 us (19%)
  Pallas kernels  6.97 us (17%)
    all_to_all x1, starting transfers between devices, local(): lax.all_to_all(words, 'slab', split_axis=0, concat_axis=0, tiled=True)  18.4 us
    all_to_all x1, waiting for transfers between devices, local(): lax.all_to_all(words, 'slab', split_axis=0, concat_axis=0, tiled=True)  8.29 us
    all_to_all x1, blocking collectives, local(): lax.all_to_all(radiance, 'disk', split_axis=0, concat_axis=0, tiled=True)  8.03 us
    pallas_call x1, Pallas kernels, local(): pl.pallas_call(prepare_kernel, out_shape=(pltpu.VMEM((KEPT, GPB, HALF, LA...  3.16 us
    pallas_call x1, Pallas kernels, local(): pl.pallas_call(pack_kernel, out_shape=pltpu.VMEM((LEVELS, LANES), jnp.int...  1.55 us
    pallas_call x1, Pallas kernels, local(): pl.pallas_call(radiate_kernel, out_shape=pltpu.VMEM((DISKS, HALF, LANES),...  1.43 us
  transfers between devices with their start and end apart: 1, of which 1 were waited for; matrix products, arithmetic and copies ran while one was open for 0% of the time, Pallas kernels for 8%

profile of v2, /device:TPU:1, one launch (start us, length us, event | category | flops | bytes accessed | tf_op | source)
XLA Modules:
  0.0 41.7 jit_solution(4884862121591935759)
XLA Ops:
  0.0 1.6 %pack.1 = s32[128,128]{1,0:T(8,128)} custom-call(f32[64,128]{1,0:T(8,128)} %bitcast.11, f32[64,128]{1,0:T(8,128)} %bitcast.12, f32[64,128]{1,0:T(8,128)} %bitcast.13), custom_call_target="tpu_custom_call" | custom-call | tf_op jit(solution)/shard_map/pack/pallas_call | solution.py:221
  1.6 18.4 %all-to-all-start = ((s32[128,1,128]{2,1,0:T(1,128)}), s32[128,1,128]{2,1,0:T(1,128)S(1)}, u32[]{:S(2)}, u32[]{:S(2)}) async-start(s32[128,1,128]{2,1,0:T(1,128)} %bitcast.4), calls=%async_computation | async-start | bytes 131072 | tf_op jit(solution)/shard_map/all_to_all | solution.py:228
  20.0 3.2 %prepare.1 = (f32[96,7,8,128]{3,2,1,0:T(8,128)S(1)}, f32[32,7,8,128]{3,2,1,0:T(8,128)}, f32[7,8,128]{2,1,0:T(8,128)S(1)}, f32[7,8,128]{2,1,0:T(8,128)S(1)}, f32[...) custom-call(f32[112,128]{1,0:T(8,128)} %mol_ref.1, f32[1,112]{1,0:T(1,128)} %bitcast.14, f32[1,112]{1,0:T(1,128)} %bitcast.15, ...), custom_call_target="tpu_custom_call" | custom-call | tf_op jit(solution)/shard_map/prepare/pallas_call | solution.py:230
  23.1 8.3 %all-to-all-done = s32[128,1,128]{2,1,0:T(1,128)S(1)} async-done(((s32[128,1,128]{2,1,0:T(1,128)}), s32[128,1,128]{2,1,0:T(1,128)S(1)}, u32[]{:S(2)}, u32[]{:S(2)}) %all-to-all-start) | async-done | bytes 65568 | tf_op jit(solution)/shard_map/all_to_all | solution.py:228
  31.4 1.4 %radiate.1 = f32[4,8,128]{2,1,0:T(8,128)S(1)} custom-call(s32[128,128]{1,0:T(8,128)S(1)} %bitcast.10, f32[96,7,8,128]{3,2,1,0:T(8,128)S(1)} %get-tuple-element.11.gas_ref, f32[32,7,8,128]{3,2,1,0:T(8,128)} %get-tuple-element.12.low_gas_ref, f32[7,8,128]{2,1,0:T(8,128)S(1)} %get-tuple-element.13.cloud_ref, f32[7,8,128]{2,1,0:T(8,128)S(1)} %get-tuple-element.14.weight_ref, ...), custom_call_target="tpu_custom_call" | custom-call | tf_op jit(solution)/shard_map/radiate/pallas_call | solution.py:250
  32.9 8.0 %all_to_all.16.rad_ref = f32[4,8,128]{2,1,0:T(8,128)S(1)} all-to-all(f32[4,8,128]{2,1,0:T(8,128)S(1)} %radiate.1), channel_id=1, replica_groups=mesh['slab'=128,'disk'=4] {'disk'}, dimensions={0} | all-to-all | bytes 32768 | tf_op jit(solution)/shard_map/all_to_all | solution.py:264
  40.9 0.8 %pixels.1 = f32[32,512]{1,0:T(8,128)} custom-call(f32[4,8,128]{2,1,0:T(8,128)S(1)} %all_to_all.16.rad_ref, bf16[256,512]{1,0:T(8,128)(2,1)S(1)} %get-tuple-element.16.mix_ref), custom_call_target="tpu_custom_call" | custom-call | tf_op jit(solution)/shard_map/pixels/pallas_call | solution.py:266
Async XLA Ops:
  1.6 29.9 %all-to-all-start = ((s32[128,1,128]{2,1,0:T(1,128)}), s32[128,1,128]{2,1,0:T(1,128)S(1)}, u32[]{:S(2)}, u32[]{:S(2)}) async-start(s32[128,1,128]{2,1,0:T(1,128)} %bitcast.4), calls=%async_computation | async-start | bytes 131072 | tf_op jit(solution)/shard_map/all_to_all | solution.py:228

commit v3 on v2

--- a/solution.py
+++ b/solution.py
@@ -16,6 +16,8 @@
 PIX = 512
 HALF = BANDS // 2
 LANES = 128
+FIRST_SLAB = 108
+FIRST_DISK = 2
 KEPT = 96
 LOG2E = 1.4426950408889634
 
@@ -27,6 +29,17 @@
 def code16(x, low, step):
     q = ((x - low) * (1.0 / step) + 0.5).astype(jnp.int32)
     return jnp.clip(q, 0, 65535)
+
+
+def swapped_group(size, first):
+    return [first if i == 0 else 0 if i == first else i for i in range(size)]
+
+
+def swap_rows(ref):
+    if FIRST_SLAB:
+        held = ref[0:1, :]
+        ref[0:1, :] = ref[FIRST_SLAB : FIRST_SLAB + 1, :]
+        ref[FIRST_SLAB : FIRST_SLAB + 1, :] = held
 
 
 def pack_kernel(temp_ref, hum_ref, con_ref, out_ref):
@@ -44,6 +57,7 @@
             moved = turn(part, (spot - dest) % 4 * COLS)
             word = moved if word is None else jnp.where(lane == spot, moved, word)
         out_ref[pl.ds(dest, rows, stride=LANES // COLS), :] = word
+    swap_rows(out_ref)
 
 
 def turn(x, shift):
@@ -141,6 +155,8 @@
     hum_ref[...] = hum.astype(jnp.float32) * HUM_STEP + HUM_LOW
     con_ref[...] = (con.astype(jnp.float32) * CON_STEP + CON_LOW) * overcast_ref[0:1, :]
     t4_ref[pl.ds(0, LEVELS), :] = t4.astype(jnp.float32) * (1.0 / T4_SCALE)
+    for by_sender in (hum_ref, con_ref, t4_ref):
+        swap_rows(by_sender)
     t4_ref[pl.ds(LEVELS, 1), :] = t4_ref[pl.ds(LEVELS - 1, 1), :]
     diff_ref[...] = t4_ref[pl.ds(1, LEVELS), :] - t4_ref[pl.ds(0, LEVELS), :]
 
@@ -176,13 +192,14 @@
 
 def pixel_kernel(rad_ref, mix_ref, out_ref):
     lane = lax.broadcasted_iota(jnp.int32, (HALF, LANES), 1) // COLS
+    sender = swapped_group(DISKS, FIRST_DISK)
     rows = []
     for hour in range(HOURS):
         for half in range(2):
             spot = half * HOURS + hour
             row = None
             for disk in range(DISKS):
-                moved = turn(rad_ref[disk], (disk - spot) % 4 * COLS)
+                moved = turn(rad_ref[sender.index(disk)], (disk - spot) % 4 * COLS)
                 row = moved if row is None else jnp.where(lane == disk, moved, row)
             rows.append(row)
     rad = jnp.concatenate(rows, axis=0).astype(jnp.bfloat16)
@@ -200,6 +217,11 @@
 
 def in_hbm(x):
     return pltpu.with_memory_space_constraint(x, pltpu.HBM)
+
+
+def exchange(x, axis, first):
+    group = swapped_group(lax.axis_size(axis), first)
+    return lax.all_to_all(x, axis, 0, 0, axis_index_groups=[group], tiled=True)
 
 
 def local(
@@ -225,7 +247,7 @@
             in_hbm(humidity_amount.reshape(rows, LANES)),
             in_hbm(slab_condensate_amount.reshape(rows, LANES)),
         )
-    words = lax.all_to_all(words, "slab", split_axis=0, concat_axis=0, tiled=True)
+    words = exchange(words, "slab", FIRST_SLAB)
     with jax.named_scope("prepare"):
         gas, low_gas, cloud, weight, overcast, mix = pl.pallas_call(
             prepare_kernel,
@@ -261,7 +283,7 @@
             ],
             compiler_params=SMALL,
         )(in_vmem(words), gas, in_hbm(low_gas), cloud, weight, overcast)
-    radiance = lax.all_to_all(radiance, "disk", split_axis=0, concat_axis=0, tiled=True)
+    radiance = exchange(radiance, "disk", FIRST_DISK)
     with jax.named_scope("pixels"):
         pixels = pl.pallas_call(
             pixel_kernel,

time: 42.1 us -> 36.4 us (0.86)
  the two profiles are of different devices: /device:TPU:1 before, /device:TPU:4 now
where the time goes in v3:
time: 36.4 us; the launch traced here: 36 us
  starting transfers between devices  19 us (52%)
  blocking collectives  7.71 us (21%)
  Pallas kernels  6.97 us (19%)
  waiting for transfers between devices  2.34 us (6%)
    all_to_all x1, starting transfers between devices, exchange(): return lax.all_to_all(x, axis, 0, 0, axis_index_groups=[group], tiled=True)  19 us
    all_to_all x1, blocking collectives, exchange(): return lax.all_to_all(x, axis, 0, 0, axis_index_groups=[group], tiled=True)  7.71 us
    pallas_call x1, Pallas kernels, local(): pl.pallas_call(prepare_kernel, out_shape=(pltpu.VMEM((KEPT, GPB, HALF, LA...  3.16 us
    all_to_all x1, waiting for transfers between devices, exchange(): return lax.all_to_all(x, axis, 0, 0, axis_index_groups=[group], tiled=True)  2.34 us
    pallas_call x1, Pallas kernels, local(): pl.pallas_call(pack_kernel, out_shape=pltpu.VMEM((LEVELS, LANES), jnp.int...  1.55 us
    pallas_call x1, Pallas kernels, local(): pl.pallas_call(radiate_kernel, out_shape=pltpu.VMEM((DISKS, HALF, LANES),...  1.43 us
    pallas_call x1, Pallas kernels, local(): pl.pallas_call(pixel_kernel, out_shape=jax.ShapeDtypeStruct((HOURS * BAND...  0.82 us
  transfers between devices with their start and end apart: 1, of which 1 were waited for; matrix products, arithmetic and copies ran while one was open for 0% of the time, Pallas kernels for 9%

profile of v3, /device:TPU:4, one launch (start us, length us, event | category | flops | bytes accessed | tf_op | source)
XLA Modules:
  0.0 36.0 jit_solution(8402680051213615855)
XLA Ops:
  0.0 1.6 %pack.1 = s32[128,128]{1,0:T(8,128)} custom-call(f32[64,128]{1,0:T(8,128)} %bitcast.11, f32[64,128]{1,0:T(8,128)} %bitcast.12, f32[64,128]{1,0:T(8,128)} %bitcast.13), custom_call_target="tpu_custom_call" | custom-call | tf_op jit(solution)/shard_map/pack/pallas_call | solution.py:243
  1.6 19.0 %all-to-all-start = ((s32[128,1,128]{2,1,0:T(1,128)}), s32[128,1,128]{2,1,0:T(1,128)S(1)}, u32[]{:S(2)}, u32[]{:S(2)}) async-start(s32[128,1,128]{2,1,0:T(1,128)} %bitcast.4), calls=%async_computation | async-start | bytes 131072 | tf_op jit(solution)/shard_map/all_to_all | solution.py:224
  20.6 3.2 %prepare.1 = (f32[96,7,8,128]{3,2,1,0:T(8,128)S(1)}, f32[32,7,8,128]{3,2,1,0:T(8,128)}, f32[7,8,128]{2,1,0:T(8,128)S(1)}, f32[7,8,128]{2,1,0:T(8,128)S(1)}, f32[...) custom-call(f32[112,128]{1,0:T(8,128)} %mol_ref.1, f32[1,112]{1,0:T(1,128)} %bitcast.14, f32[1,112]{1,0:T(1,128)} %bitcast.15, ...), custom_call_target="tpu_custom_call" | custom-call | tf_op jit(solution)/shard_map/prepare/pallas_call | solution.py:252
  23.7 2.3 %all-to-all-done = s32[128,1,128]{2,1,0:T(1,128)S(1)} async-done(((s32[128,1,128]{2,1,0:T(1,128)}), s32[128,1,128]{2,1,0:T(1,128)S(1)}, u32[]{:S(2)}, u32[]{:S(2)}) %all-to-all-start) | async-done | bytes 65568 | tf_op jit(solution)/shard_map/all_to_all | solution.py:224
  26.1 1.4 %radiate.1 = f32[4,8,128]{2,1,0:T(8,128)S(1)} custom-call(s32[128,128]{1,0:T(8,128)S(1)} %bitcast.10, f32[96,7,8,128]{3,2,1,0:T(8,128)S(1)} %get-tuple-element.11.gas_ref, f32[32,7,8,128]{3,2,1,0:T(8,128)} %get-tuple-element.12.low_gas_ref, f32[7,8,128]{2,1,0:T(8,128)S(1)} %get-tuple-element.13.cloud_ref, f32[7,8,128]{2,1,0:T(8,128)S(1)} %get-tuple-element.14.weight_ref, ...), custom_call_target="tpu_custom_call" | custom-call | tf_op jit(solution)/shard_map/radiate/pallas_call | solution.py:272
  27.5 7.7 %all_to_all.16.rad_ref = f32[4,8,128]{2,1,0:T(8,128)S(1)} all-to-all(f32[4,8,128]{2,1,0:T(8,128)S(1)} %radiate.1), channel_id=1, replica_groups={{2,1,0,3},{6,5,4,7},{10,9,8,11},{14,13,12,15},{18,17,16,19},{22,21,20,2..., dimensions={0} | all-to-all | bytes 32768 | tf_op jit(solution)/shard_map/all_to_all | solution.py:224
  35.2 0.8 %pixels.1 = f32[32,512]{1,0:T(8,128)} custom-call(f32[4,8,128]{2,1,0:T(8,128)S(1)} %all_to_all.16.rad_ref, bf16[256,512]{1,0:T(8,128)(2,1)S(1)} %get-tuple-element.16.mix_ref), custom_call_target="tpu_custom_call" | custom-call | tf_op jit(solution)/shard_map/pixels/pallas_call | solution.py:288
Async XLA Ops:
  1.6 24.5 %all-to-all-start = ((s32[128,1,128]{2,1,0:T(1,128)}), s32[128,1,128]{2,1,0:T(1,128)S(1)}, u32[]{:S(2)}, u32[]{:S(2)}) async-start(s32[128,1,128]{2,1,0:T(1,128)} %bitcast.4), calls=%async_computation | async-start | bytes 131072 | tf_op jit(solution)/shard_map/all_to_all | solution.py:224

commit v4 on v3

--- a/solution.py
+++ b/solution.py
@@ -16,9 +16,9 @@
 PIX = 512
 HALF = BANDS // 2
 LANES = 128
-FIRST_SLAB = 108
+FIRST_SLAB = 75
 FIRST_DISK = 2
-KEPT = 96
+EARLY = 3
 LOG2E = 1.4426950408889634
 
 HUM_LOW, HUM_STEP = 0.2, 1.8 / 65535.0
@@ -42,15 +42,33 @@
         ref[FIRST_SLAB : FIRST_SLAB + 1, :] = held
 
 
-def pack_kernel(temp_ref, hum_ref, con_ref, out_ref):
+def turn(x, shift):
+    return x if isinstance(shift, int) and shift == 0 else pltpu.roll(x, shift, 1)
+
+
+def is_early():
+    return lax.rem(lax.axis_index("slab") // 2, 8) < EARLY
+
+
+def fetch(pairs, sem_ref):
+    copies = [pltpu.make_async_copy(src, dst, sem_ref.at[k]) for k, (src, dst) in enumerate(pairs)]
+    for copy in copies:
+        copy.start()
+    return copies
+
+
+def pack(temp_ref, hum_ref, con_ref, copies, out_ref):
     rows = SECTOR // LANES
+    lane = lax.broadcasted_iota(jnp.int32, (rows, LANES), 1) // COLS
+    copies[0].wait()
     t2 = temp_ref[...] * temp_ref[...]
     t4 = (t2 * t2 * T4_SCALE).astype(jnp.int32)
+    copies[1].wait()
     hum = code16(hum_ref[...], HUM_LOW, HUM_STEP)
+    copies[2].wait()
     con = code16(con_ref[...], CON_LOW, CON_STEP)
     gas = (hum << 16) | con
     parts = (gas[:rows], gas[rows:], t4[:rows], t4[rows:])
-    lane = lax.broadcasted_iota(jnp.int32, (rows, LANES), 1) // COLS
     for dest in range(LANES // COLS):
         word = None
         for spot, part in enumerate(parts):
@@ -60,14 +78,15 @@
     swap_rows(out_ref)
 
 
-def turn(x, shift):
-    return x if isinstance(shift, int) and shift == 0 else pltpu.roll(x, shift, 1)
-
-
-def prepare_kernel(
-    mol_ref, con_ref, planck_ref, over_ref, source_ref, factor_ref,
-    gas_ref, low_gas_ref, cloud_ref, weight_ref, overcast_ref, mix_ref,
-):
+def spread(mol_hbm, con_hbm, planck_hbm, over_hbm, gas_ref, cloud_ref, weight_ref, overcast_ref, room):
+    mol_ref, con_ref, planck_ref, over_ref, sem_ref = room
+    strip = lax.axis_index("slab")
+    group = LANES // COLS
+    block = over_hbm.at[:, pl.ds(pl.multiple_of(strip // group * LANES, LANES), LANES)]
+    for copy in fetch(
+        ((mol_hbm, mol_ref), (con_hbm, con_ref), (planck_hbm, planck_ref), (block, over_ref)), sem_ref
+    ):
+        copy.wait()
     lane = lax.broadcasted_iota(jnp.int32, (HALF, LANES), 1)
     first = lane < LANES // 2
     con = jnp.broadcast_to(con_ref[...], (HALF, con_ref.shape[1]))
@@ -88,6 +107,13 @@
         cloud_ref[j] = column(con, j) * -LOG2E
         weight_ref[j] = column(planck, j)
 
+    overcast = None
+    for spot in range(group):
+        row = jnp.broadcast_to(over_ref[spot % HOURS : spot % HOURS + 1, :], (HALF, LANES))
+        row = pltpu.roll(row, (spot - strip % group + group) % group * COLS, 1)
+        overcast = row if overcast is None else jnp.where(lane // COLS == spot, row, overcast)
+    overcast_ref[...] = overcast.astype(jnp.float32)
+
     span = LANES // 4
     shape = (span * HALF, LANES)
     pick = lax.broadcasted_iota(jnp.int32, shape, 1) % span == (
@@ -96,7 +122,7 @@
     half_of = lambda axis: lax.broadcasted_iota(jnp.int32, (LANES, LANES), axis) // (LANES // 2)
     same_half = (half_of(0) == half_of(1)).astype(jnp.float32).astype(jnp.bfloat16)
 
-    def levels(q, first_level, to_ref):
+    def levels(q, _):
         for j in range(GPB):
             row = None
             for half in range(2):
@@ -109,23 +135,17 @@
             rows = jnp.broadcast_to(row[None], (span, HALF, LANES)).reshape(shape)
             rows = jnp.where(pick, rows, 0.0).astype(jnp.bfloat16)
             wide = jnp.dot(rows, same_half, preferred_element_type=jnp.float32)
-            start = pl.multiple_of(first_level, span)
-            to_ref[pl.ds(start, span), j] = wide.reshape(span, HALF, LANES)
+            start = pl.multiple_of(q * span, span)
+            gas_ref[pl.ds(start, span), j] = wide.reshape(span, HALF, LANES)
         return 0
 
-    levels(KEPT // span, 0, low_gas_ref)
-    lax.fori_loop(0, KEPT // span, lambda q, _: levels(q, q * span, gas_ref), 0)
-
-    strip = lax.axis_index("slab")
-    group = LANES // COLS
-    block = over_ref[:, pl.ds(pl.multiple_of(strip // group * LANES, LANES), LANES)]
-    overcast = None
-    for spot in range(group):
-        row = jnp.broadcast_to(block[spot % HOURS : spot % HOURS + 1], (HALF, LANES))
-        row = pltpu.roll(row, (spot - strip % group + group) % group * COLS, 1)
-        overcast = row if overcast is None else jnp.where(lane // COLS == spot, row, overcast)
-    overcast_ref[...] = overcast.astype(jnp.float32)
-
+    lax.fori_loop(0, 4, levels, 0)
+
+
+def blend(source_hbm, factor_hbm, mix_ref, room):
+    source_ref, factor_ref, sem_ref = room
+    for copy in fetch(((source_hbm, source_ref), (factor_hbm, factor_ref)), sem_ref):
+        copy.wait()
     strip_cols = DISKS * COLS
     col = lax.broadcasted_iota(jnp.int32, (strip_cols, PIX), 0)
     source = source_ref[...]
@@ -138,13 +158,25 @@
     mix_ref[pl.ds(strip_cols, strip_cols), :] = (mix - high.astype(jnp.float32)).astype(jnp.bfloat16)
 
 
-def radiate_kernel(
-    word_ref, gas_ref, low_gas_ref, cloud_ref, weight_ref, overcast_ref,
-    out_ref,
-    tail_ref, hum_ref, con_ref, t4_ref, diff_ref, sem,
+def pack_kernel(
+    temp_hbm, hum_hbm, con_hbm, mol_hbm, cond_hbm, planck_hbm, over_hbm, source_hbm, factor_hbm,
+    word_ref, gas_ref, cloud_ref, weight_ref, overcast_ref, mix_ref,
+    temp_ref, hum_ref, con_ref, field_sem, *room,
 ):
-    copy = pltpu.make_async_copy(low_gas_ref, tail_ref, sem)
-    copy.start()
+    fields = (temp_hbm, temp_ref), (hum_hbm, hum_ref), (con_hbm, con_ref)
+    pack(temp_ref, hum_ref, con_ref, fetch(fields, field_sem), word_ref)
+
+    @pl.when(is_early())
+    def _():
+        spread(
+            mol_hbm, cond_hbm, planck_hbm, over_hbm,
+            gas_ref, cloud_ref, weight_ref, overcast_ref, room[:5],
+        )
+        blend(source_hbm, factor_hbm, mix_ref, room[5:])
+
+
+def radiate(word_ref, gas_ref, cloud_ref, weight_ref, overcast_ref, out_ref, rows):
+    hum_ref, con_ref, t4_ref, diff_ref = rows
     word = word_ref[...]
     swapped = pltpu.roll(word, LANES // 2, 1)
     first = lax.broadcasted_iota(jnp.int32, word.shape, 1) < LANES // 2
@@ -163,24 +195,19 @@
     zero = jnp.zeros((HALF, LANES), jnp.float32)
     clouds = [cloud_ref[j] for j in range(GPB)]
 
-    def step(i, carry, from_ref, start):
+    def step(i, carry):
         depth, total = list(carry[0]), list(carry[1])
         for k in range(8):
             level = 8 * i + k
-            hum_row = hum_ref[pl.ds(start + level, HALF, stride=0), :]
-            con_row = con_ref[pl.ds(start + level, HALF, stride=0), :]
-            diff_row = diff_ref[pl.ds(start + level, HALF, stride=0), :]
+            hum_row = hum_ref[pl.ds(level, HALF, stride=0), :]
+            con_row = con_ref[pl.ds(level, HALF, stride=0), :]
+            diff_row = diff_ref[pl.ds(level, HALF, stride=0), :]
             for j in range(GPB):
-                depth[j] = depth[j] + (from_ref[level, j] * hum_row + clouds[j] * con_row)
+                depth[j] = depth[j] + (gas_ref[level, j] * hum_row + clouds[j] * con_row)
                 total[j] = total[j] + diff_row * jnp.exp2(depth[j])
         return tuple(depth), tuple(total)
 
-    carry = (zero,) * GPB, (zero,) * GPB
-    carry = lax.fori_loop(0, KEPT // 8, lambda i, c: step(i, c, gas_ref, 0), carry)
-    copy.wait()
-    _, total = lax.fori_loop(
-        0, (LEVELS - KEPT) // 8, lambda i, c: step(i, c, tail_ref, KEPT), carry
-    )
+    _, total = lax.fori_loop(0, LEVELS // 8, step, ((zero,) * GPB, (zero,) * GPB))
     top = t4_ref[pl.ds(0, HALF, stride=0), :]
     band = zero
     for j in range(GPB):
@@ -190,7 +217,25 @@
         out_ref[owner] = band
 
 
-def pixel_kernel(rad_ref, mix_ref, out_ref):
+def radiate_kernel(
+    word_ref, gas_ref, cloud_ref, weight_ref, overcast_ref, mol_hbm, cond_hbm, planck_hbm, over_hbm,
+    out_ref,
+    own_gas, own_cloud, own_weight, own_overcast, hum_ref, con_ref, t4_ref, diff_ref, *room,
+):
+    rows = hum_ref, con_ref, t4_ref, diff_ref
+
+    @pl.when(is_early())
+    def _():
+        radiate(word_ref, gas_ref, cloud_ref, weight_ref, overcast_ref, out_ref, rows)
+
+    @pl.when(jnp.logical_not(is_early()))
+    def _():
+        own = own_gas, own_cloud, own_weight, own_overcast
+        spread(mol_hbm, cond_hbm, planck_hbm, over_hbm, *own, room)
+        radiate(word_ref, *own, out_ref, rows)
+
+
+def pixel_kernel(rad_ref, mix_ref, source_hbm, factor_hbm, out_ref, own_mix, *room):
     lane = lax.broadcasted_iota(jnp.int32, (HALF, LANES), 1) // COLS
     sender = swapped_group(DISKS, FIRST_DISK)
     rows = []
@@ -204,11 +249,20 @@
             rows.append(row)
     rad = jnp.concatenate(rows, axis=0).astype(jnp.bfloat16)
     rad = jnp.concatenate([rad, rad], axis=1)
-    out_ref[...] = jnp.dot(rad, mix_ref[...], preferred_element_type=jnp.float32)
+
+    @pl.when(is_early())
+    def _():
+        out_ref[...] = jnp.dot(rad, mix_ref[...], preferred_element_type=jnp.float32)
+
+    @pl.when(jnp.logical_not(is_early()))
+    def _():
+        blend(source_hbm, factor_hbm, own_mix, room)
+        out_ref[...] = jnp.dot(rad, own_mix[...], preferred_element_type=jnp.float32)
 
 
 ANY = pl.BlockSpec(memory_space=pl.ANY)
-SMALL = pltpu.CompilerParams(vmem_limit_bytes=8 << 20)
+WHOLE = pl.BlockSpec(memory_space=pltpu.VMEM)
+SMALL = pltpu.CompilerParams(vmem_limit_bytes=16 << 20)
 
 
 def in_vmem(x):
@@ -237,59 +291,72 @@
 ):
     f32 = jnp.float32
     rows = HOURS * SECTOR // LANES
+    field = pltpu.VMEM((rows, LANES), f32)
     level_cols = pltpu.VMEM((LEVELS, LANES), f32)
     per_point = pltpu.VMEM((GPB, HALF, LANES), f32)
+    prepared = [
+        pltpu.VMEM((LEVELS, GPB, HALF, LANES), f32),
+        per_point,
+        per_point,
+        pltpu.VMEM((HALF, LANES), f32),
+    ]
+    mixed = pltpu.VMEM((2 * DISKS * COLS, PIX), jnp.bfloat16)
+    points = condensate_opacity.shape[0]
+    spread_room = [
+        pltpu.VMEM((points, LEVELS), f32),
+        pltpu.VMEM((1, points), f32),
+        pltpu.VMEM((1, points), f32),
+        pltpu.VMEM((HOURS, LANES), jnp.int32),
+        pltpu.SemaphoreType.DMA((4,)),
+    ]
+    blend_room = [
+        pltpu.VMEM((TAPS, PIX), jnp.int32),
+        pltpu.VMEM((TAPS, PIX), f32),
+        pltpu.SemaphoreType.DMA((2,)),
+    ]
+    opacities = [
+        in_hbm(molecular_opacity),
+        in_hbm(condensate_opacity.reshape(1, -1)),
+        in_hbm(planck_quadrature_factor.reshape(1, -1)),
+        in_hbm(overcast_indicator),
+    ]
+    scene = [in_hbm(scene_contributing_profiles), in_hbm(scene_interpolation_factors)]
     with jax.named_scope("pack"):
-        words = pl.pallas_call(
-            pack_kernel, out_shape=pltpu.VMEM((LEVELS, LANES), jnp.int32), compiler_params=SMALL
+        words, *ready, mix = pl.pallas_call(
+            pack_kernel,
+            out_shape=(pltpu.VMEM((LEVELS, LANES), jnp.int32), *prepared, mixed),
+            in_specs=[ANY] * 9,
+            out_specs=[WHOLE] * 6,
+            scratch_shapes=[field] * 3 + [pltpu.SemaphoreType.DMA((3,))] + spread_room + blend_room,
+            compiler_params=SMALL,
         )(
             in_hbm(thermal_anomaly.reshape(rows, LANES)),
             in_hbm(humidity_amount.reshape(rows, LANES)),
             in_hbm(slab_condensate_amount.reshape(rows, LANES)),
+            *opacities,
+            *scene,
         )
     words = exchange(words, "slab", FIRST_SLAB)
-    with jax.named_scope("prepare"):
-        gas, low_gas, cloud, weight, overcast, mix = pl.pallas_call(
-            prepare_kernel,
-            out_shape=(
-                pltpu.VMEM((KEPT, GPB, HALF, LANES), f32),
-                pltpu.HBM((LEVELS - KEPT, GPB, HALF, LANES), f32),
-                per_point,
-                per_point,
-                pltpu.VMEM((HALF, LANES), f32),
-                pltpu.VMEM((2 * DISKS * COLS, PIX), jnp.bfloat16),
-            ),
-            compiler_params=SMALL,
-        )(
-            in_hbm(molecular_opacity),
-            in_hbm(condensate_opacity.reshape(1, -1)),
-            in_hbm(planck_quadrature_factor.reshape(1, -1)),
-            in_hbm(overcast_indicator),
-            in_hbm(scene_contributing_profiles),
-            in_hbm(scene_interpolation_factors),
-        )
     with jax.named_scope("radiate"):
         radiance = pl.pallas_call(
             radiate_kernel,
             out_shape=pltpu.VMEM((DISKS, HALF, LANES), f32),
-            in_specs=[ANY if k == 2 else pl.BlockSpec() for k in range(6)],
-            scratch_shapes=[
-                pltpu.VMEM((LEVELS - KEPT, GPB, HALF, LANES), f32),
-                level_cols,
-                level_cols,
-                pltpu.VMEM((LEVELS + 8, LANES), f32),
-                level_cols,
-                pltpu.SemaphoreType.DMA,
-            ],
+            in_specs=[WHOLE] * 5 + [ANY] * 4,
+            out_specs=WHOLE,
+            scratch_shapes=prepared
+            + [level_cols, level_cols, pltpu.VMEM((LEVELS + 8, LANES), f32), level_cols]
+            + spread_room,
             compiler_params=SMALL,
-        )(in_vmem(words), gas, in_hbm(low_gas), cloud, weight, overcast)
+        )(in_vmem(words), *ready, *opacities)
     radiance = exchange(radiance, "disk", FIRST_DISK)
     with jax.named_scope("pixels"):
         pixels = pl.pallas_call(
             pixel_kernel,
             out_shape=jax.ShapeDtypeStruct((HOURS * BANDS, PIX), f32),
+            in_specs=[WHOLE] * 2 + [ANY] * 2,
+            scratch_shapes=[mixed] + blend_room,
             compiler_params=SMALL,
-        )(in_vmem(radiance), mix)
+        )(in_vmem(radiance), mix, *scene)
     return pixels.reshape(HOURS, BANDS, PIX)
 
 

time: 36.4 us -> 34.1 us (0.937)
  blocking collectives: 7.71 us -> 28 us
  starting transfers between devices: 19 us -> 0 us
  waiting for transfers between devices: 2.34 us -> 0 us
  Pallas kernels: 6.97 us -> 5.82 us
    all_to_all x1 -> x2, blocking collectives: 7.71 us -> 28 us  [exchange(): return lax.all_to_all(x, axis, 0, 0, axis_index_groups=[group], tiled=True)]
    all_to_all x1 -> x0, starting transfers between devices: 19 us -> none  [exchange(): return lax.all_to_all(x, axis, 0, 0, axis_index_groups=[group], tiled=True)]
    all_to_all x1 -> x0, waiting for transfers between devices: 2.34 us -> none  [exchange(): return lax.all_to_all(x, axis, 0, 0, axis_index_groups=[group], tiled=True)]
    pallas_call x2 -> x1, Pallas kernels: 4.71 us -> 3.85 us  [local(): pl.pallas_call(pack_kernel, out_shape=(pltpu.VMEM((LEVELS, LANES), jnp.in...]
  transfers between devices with their start and end apart: 1 -> 0, of which waited for: 1 -> 0; matrix products, arithmetic and copies ran while one was open for 0% -> 0% of each run, Pallas kernels for 9% -> 0%
where the time goes in v4:
time: 34.1 us; the launch traced here: 33.8 us
  blocking collectives  28 us (82%)
  Pallas kernels  5.82 us (17%)
    all_to_all x2, blocking collectives, exchange(): return lax.all_to_all(x, axis, 0, 0, axis_index_groups=[group], tiled=True)  28 us
    pallas_call x1, Pallas kernels, local(): pl.pallas_call(pack_kernel, out_shape=(pltpu.VMEM((LEVELS, LANES), jnp.in...  3.85 us
    pallas_call x1, Pallas kernels, local(): pl.pallas_call(radiate_kernel, out_shape=pltpu.VMEM((DISKS, HALF, LANES),...  1.11 us
    pallas_call x1, Pallas kernels, local(): pl.pallas_call(pixel_kernel, out_shape=jax.ShapeDtypeStruct((HOURS * BAND...  0.86 us

profile of v4, /device:TPU:4, one launch (start us, length us, event | category | flops | bytes accessed | tf_op | source)
XLA Modules:
  0.0 33.8 jit_solution(2794835735155360063)
XLA Ops:
  0.0 3.9 %pack.1 = (s32[128,128]{1,0:T(8,128)S(1)}, f32[128,7,8,128]{3,2,1,0:T(8,128)S(1)}, f32[7,8,128]{2,1,0:T(8,128)S(1)}, f32[7,8,128]{2,1,0:T(8,128)S(1)}, f32[8,128...) custom-call(f32[64,128]{1,0:T(8,128)} %bitcast.12, f32[64,128]{1,0:T(8,128)} %bitcast.13, f32[64,128]{1,0:T(8,128)} %bitcast.14, ...), custom_call_target="tpu_custom_call" | custom-call | tf_op jit(solution)/shard_map/pack/pallas_call | solution.py:325
  3.9 20.0 %all_to_all.16 = s32[128,1,128]{2,1,0:T(1,128)S(1)} all-to-all(s32[128,1,128]{2,1,0:T(1,128)S(1)} %bitcast.11), channel_id=1, replica_groups={{300,4,8,12,16,20,24,28,32,36,40,44,48,52,56,60,64,68,72,76,80,84,88,92..., dimensions={0} | all-to-all | bytes 131072 | tf_op jit(solution)/shard_map/all_to_all | solution.py:278
  23.8 1.1 %radiate.1 = f32[4,8,128]{2,1,0:T(8,128)S(1)} custom-call(s32[128,128]{1,0:T(8,128)S(1)} %bitcast.10, f32[128,7,8,128]{3,2,1,0:T(8,128)S(1)} %get-tuple-element.12.gas_ref, f32[7,8,128]{2,1,0:T(8,128)S(1)} %get-tuple-element.13.cloud_ref, f32[7,8,128]{2,1,0:T(8,128)S(1)} %get-tuple-element.14.weight_ref, f32[8,128]{1,0:T(8,128)S(1)} %get-tuple-element.15.overcast_ref, ...), custom_call_target="tpu_custom_call" | custom-call | tf_op jit(solution)/shard_map/radiate/pallas_call | solution.py:341
  24.9 8.0 %all_to_all.17.rad_ref = f32[4,8,128]{2,1,0:T(8,128)S(1)} all-to-all(f32[4,8,128]{2,1,0:T(8,128)S(1)} %radiate.1), channel_id=1, replica_groups={{2,1,0,3},{6,5,4,7},{10,9,8,11},{14,13,12,15},{18,17,16,19},{22,21,20,2..., dimensions={0} | all-to-all | bytes 32768 | tf_op jit(solution)/shard_map/all_to_all | solution.py:278
  33.0 0.9 %pixels.1 = f32[32,512]{1,0:T(8,128)} custom-call(f32[4,8,128]{2,1,0:T(8,128)S(1)} %all_to_all.17.rad_ref, bf16[256,512]{1,0:T(8,128)(2,1)S(1)} %get-tuple-element.16.mix_ref, s32[4,512]{1,0:T(4,128)} %source_hbm.3, f32[4,512]{1,0:T(4,128)} %factor_hbm.3), custom_call_target="tpu_custom_call" | custom-call | tf_op jit(solution)/shard_map/pixels/pallas_call | solution.py:353

commit v5 on v4

--- a/solution.py
+++ b/solution.py
@@ -19,6 +19,7 @@
 FIRST_SLAB = 75
 FIRST_DISK = 2
 EARLY = 3
+STEP = 32
 LOG2E = 1.4426950408889634
 
 HUM_LOW, HUM_STEP = 0.2, 1.8 / 65535.0
@@ -78,7 +79,7 @@
     swap_rows(out_ref)
 
 
-def spread(mol_hbm, con_hbm, planck_hbm, over_hbm, gas_ref, cloud_ref, weight_ref, overcast_ref, room):
+def spread(mol_hbm, con_hbm, planck_hbm, over_hbm, gas_ref, cloud_ref, start_ref, weight_ref, overcast_ref, room):
     mol_ref, con_ref, planck_ref, over_ref, sem_ref = room
     strip = lax.axis_index("slab")
     group = LANES // COLS
@@ -105,7 +106,10 @@
 
     for j in range(GPB):
         cloud_ref[j] = column(con, j) * -LOG2E
-        weight_ref[j] = column(planck, j)
+        weight = column(planck, j)
+        start_ref[j] = jnp.log(weight) * LOG2E
+        total = weight if j == 0 else total + weight
+    weight_ref[...] = total
 
     overcast = None
     for spot in range(group):
@@ -160,7 +164,7 @@
 
 def pack_kernel(
     temp_hbm, hum_hbm, con_hbm, mol_hbm, cond_hbm, planck_hbm, over_hbm, source_hbm, factor_hbm,
-    word_ref, gas_ref, cloud_ref, weight_ref, overcast_ref, mix_ref,
+    word_ref, gas_ref, cloud_ref, start_ref, weight_ref, overcast_ref, mix_ref,
     temp_ref, hum_ref, con_ref, field_sem, *room,
 ):
     fields = (temp_hbm, temp_ref), (hum_hbm, hum_ref), (con_hbm, con_ref)
@@ -170,12 +174,12 @@
     def _():
         spread(
             mol_hbm, cond_hbm, planck_hbm, over_hbm,
-            gas_ref, cloud_ref, weight_ref, overcast_ref, room[:5],
+            gas_ref, cloud_ref, start_ref, weight_ref, overcast_ref, room[:5],
         )
         blend(source_hbm, factor_hbm, mix_ref, room[5:])
 
 
-def radiate(word_ref, gas_ref, cloud_ref, weight_ref, overcast_ref, out_ref, rows):
+def radiate(word_ref, gas_ref, cloud_ref, start_ref, weight_ref, overcast_ref, out_ref, rows):
     hum_ref, con_ref, t4_ref, diff_ref = rows
     word = word_ref[...]
     swapped = pltpu.roll(word, LANES // 2, 1)
@@ -192,45 +196,45 @@
     t4_ref[pl.ds(LEVELS, 1), :] = t4_ref[pl.ds(LEVELS - 1, 1), :]
     diff_ref[...] = t4_ref[pl.ds(1, LEVELS), :] - t4_ref[pl.ds(0, LEVELS), :]
 
-    zero = jnp.zeros((HALF, LANES), jnp.float32)
     clouds = [cloud_ref[j] for j in range(GPB)]
 
     def step(i, carry):
-        depth, total = list(carry[0]), list(carry[1])
-        for k in range(8):
-            level = 8 * i + k
+        depth, total = list(carry[0]), carry[1]
+        for k in range(STEP):
+            level = STEP * i + k
             hum_row = hum_ref[pl.ds(level, HALF, stride=0), :]
             con_row = con_ref[pl.ds(level, HALF, stride=0), :]
             diff_row = diff_ref[pl.ds(level, HALF, stride=0), :]
             for j in range(GPB):
                 depth[j] = depth[j] + (gas_ref[level, j] * hum_row + clouds[j] * con_row)
-                total[j] = total[j] + diff_row * jnp.exp2(depth[j])
-        return tuple(depth), tuple(total)
-
-    _, total = lax.fori_loop(0, LEVELS // 8, step, ((zero,) * GPB, (zero,) * GPB))
+            seen = [jnp.exp2(x) for x in depth]
+            while len(seen) > 1:
+                seen = [a + b for a, b in zip(seen[::2], seen[1::2])] + seen[len(seen) // 2 * 2 :]
+            total = total + diff_row * seen[0]
+        return tuple(depth), total
+
+    starts = tuple(start_ref[j] for j in range(GPB))
+    _, total = lax.fori_loop(0, LEVELS // STEP, step, (starts, jnp.zeros((HALF, LANES), jnp.float32)))
     top = t4_ref[pl.ds(0, HALF, stride=0), :]
-    band = zero
-    for j in range(GPB):
-        band = band + weight_ref[j] * (top + total[j])
-    band = (band / GPB).astype(jnp.bfloat16).astype(jnp.float32)
+    band = ((weight_ref[...] * top + total) / GPB).astype(jnp.bfloat16)
     for owner in range(DISKS):
         out_ref[owner] = band
 
 
 def radiate_kernel(
-    word_ref, gas_ref, cloud_ref, weight_ref, overcast_ref, mol_hbm, cond_hbm, planck_hbm, over_hbm,
+    word_ref, gas_ref, cloud_ref, start_ref, weight_ref, overcast_ref, mol_hbm, cond_hbm, planck_hbm, over_hbm,
     out_ref,
-    own_gas, own_cloud, own_weight, own_overcast, hum_ref, con_ref, t4_ref, diff_ref, *room,
+    own_gas, own_cloud, own_start, own_weight, own_overcast, hum_ref, con_ref, t4_ref, diff_ref, *room,
 ):
     rows = hum_ref, con_ref, t4_ref, diff_ref
 
     @pl.when(is_early())
     def _():
-        radiate(word_ref, gas_ref, cloud_ref, weight_ref, overcast_ref, out_ref, rows)
+        radiate(word_ref, gas_ref, cloud_ref, start_ref, weight_ref, overcast_ref, out_ref, rows)
 
     @pl.when(jnp.logical_not(is_early()))
     def _():
-        own = own_gas, own_cloud, own_weight, own_overcast
+        own = own_gas, own_cloud, own_start, own_weight, own_overcast
         spread(mol_hbm, cond_hbm, planck_hbm, over_hbm, *own, room)
         radiate(word_ref, *own, out_ref, rows)
 
@@ -244,7 +248,7 @@
             spot = half * HOURS + hour
             row = None
             for disk in range(DISKS):
-                moved = turn(rad_ref[sender.index(disk)], (disk - spot) % 4 * COLS)
+                moved = turn(rad_ref[sender.index(disk)].astype(jnp.float32), (disk - spot) % 4 * COLS)
                 row = moved if row is None else jnp.where(lane == disk, moved, row)
             rows.append(row)
     rad = jnp.concatenate(rows, axis=0).astype(jnp.bfloat16)
@@ -298,6 +302,7 @@
         pltpu.VMEM((LEVELS, GPB, HALF, LANES), f32),
         per_point,
         per_point,
+        pltpu.VMEM((HALF, LANES), f32),
         pltpu.VMEM((HALF, LANES), f32),
     ]
     mixed = pltpu.VMEM((2 * DISKS * COLS, PIX), jnp.bfloat16)
@@ -326,7 +331,7 @@
             pack_kernel,
             out_shape=(pltpu.VMEM((LEVELS, LANES), jnp.int32), *prepared, mixed),
             in_specs=[ANY] * 9,
-            out_specs=[WHOLE] * 6,
+            out_specs=[WHOLE] * 7,
             scratch_shapes=[field] * 3 + [pltpu.SemaphoreType.DMA((3,))] + spread_room + blend_room,
             compiler_params=SMALL,
         )(
@@ -340,8 +345,8 @@
     with jax.named_scope("radiate"):
         radiance = pl.pallas_call(
             radiate_kernel,
-            out_shape=pltpu.VMEM((DISKS, HALF, LANES), f32),
-            in_specs=[WHOLE] * 5 + [ANY] * 4,
+            out_shape=pltpu.VMEM((DISKS, HALF, LANES), jnp.bfloat16),
+            in_specs=[WHOLE] * 6 + [ANY] * 4,
             out_specs=WHOLE,
             scratch_shapes=prepared
             + [level_cols, level_cols, pltpu.VMEM((LEVELS + 8, LANES), f32), level_cols]

time: 34.1 us -> 33.9 us (level)
  the two profiles are of different devices: /device:TPU:4 before, /device:TPU:8 now
where the time goes in v5:
time: 33.9 us; the launch traced here: 33.6 us
  blocking collectives  27.9 us (82%)
  Pallas kernels  5.64 us (17%)
    all_to_all x2, blocking collectives, exchange(): return lax.all_to_all(x, axis, 0, 0, axis_index_groups=[group], tiled=True)  27.9 us
    pallas_call x1, Pallas kernels, local(): pl.pallas_call(pack_kernel, out_shape=(pltpu.VMEM((LEVELS, LANES), jnp.in...  3.85 us
    pallas_call x1, Pallas kernels, local(): pl.pallas_call(radiate_kernel, out_shape=pltpu.VMEM((DISKS, HALF, LANES),...  0.92 us
    pallas_call x1, Pallas kernels, local(): pl.pallas_call(pixel_kernel, out_shape=jax.ShapeDtypeStruct((HOURS * BAND...  0.87 us

profile of v5, /device:TPU:8, one launch (start us, length us, event | category | flops | bytes accessed | tf_op | source)
XLA Modules:
  0.0 33.6 jit_solution(14136724156682790191)
XLA Ops:
  0.0 3.9 %pack.1 = (s32[128,128]{1,0:T(8,128)S(1)}, f32[128,7,8,128]{3,2,1,0:T(8,128)S(1)}, f32[7,8,128]{2,1,0:T(8,128)S(1)}, f32[7,8,128]{2,1,0:T(8,128)S(1)}, f32[8,128...) custom-call(f32[64,128]{1,0:T(8,128)} %bitcast.12, f32[64,128]{1,0:T(8,128)} %bitcast.13, ...), custom_call_target="tpu_custom_call" | custom-call | tf_op jit(solution)/shard_map/pack/pallas_call | solution.py:330
  3.9 21.0 %all_to_all.16 = s32[128,1,128]{2,1,0:T(1,128)S(1)} all-to-all(s32[128,1,128]{2,1,0:T(1,128)S(1)} %bitcast.11), channel_id=1, replica_groups={{300,4,8,12,16,20,24,28,32,36,40,44,48,52,56,60,64,68,72,76,80,84,88,92..., dimensions={0} | all-to-all | bytes 131072 | tf_op jit(solution)/shard_map/all_to_all | solution.py:282
  24.9 0.9 %radiate.1 = bf16[4,8,128]{2,1,0:T(8,128)(2,1)S(1)} custom-call(s32[128,128]{1,0:T(8,128)S(1)} %bitcast.10, f32[128,7,8,128]{3,2,1,0:T(8,128)S(1)} %get-tuple-element.13.gas_ref, f32[7,8,128]{2,1,0:T(8,128)S(1)} %get-tuple-element.14.cloud_ref, f32[7,8,128]{2,1,0:T(8,128)S(1)} %get-tuple-element.15.start_ref, f32[8,128]{1,0:T(8,128)S(1)} %get-tuple-element.16.weight_ref, ...), custom_call_target="tpu_custom_call" | custom-call | tf_op jit(solution)/shard_map/radiate/pallas_call | solution.py:346
  25.8 6.9 %all_to_all.17.rad_ref = bf16[4,8,128]{2,1,0:T(8,128)(2,1)S(1)} all-to-all(bf16[4,8,128]{2,1,0:T(8,128)(2,1)S(1)} %radiate.1), channel_id=1, replica_groups={{2,1,0,3},{6,5,4,7},{10,9,8,11},{14,13,12,15},{18,17,16,19},{22,21,20,2..., dimensions={0} | all-to-all | bytes 16384 | tf_op jit(solution)/shard_map/all_to_all | solution.py:282
  32.7 0.9 %pixels.1 = f32[32,512]{1,0:T(8,128)} custom-call(bf16[4,8,128]{2,1,0:T(8,128)(2,1)S(1)} %all_to_all.17.rad_ref, bf16[256,512]{1,0:T(8,128)(2,1)S(1)} %get-tuple-element.18.mix_ref, s32[4,512]{1,0:T(4,128)} %source_hbm.3, f32[4,512]{1,0:T(4,128)} %factor_hbm.3), custom_call_target="tpu_custom_call" | custom-call | tf_op jit(solution)/shard_map/pixels/pallas_call | solution.py:358

commit v6 on v5

--- a/solution.py
+++ b/solution.py
@@ -19,7 +19,7 @@
 FIRST_SLAB = 75
 FIRST_DISK = 2
 EARLY = 3
-STEP = 32
+STEP = 128
 LOG2E = 1.4426950408889634
 
 HUM_LOW, HUM_STEP = 0.2, 1.8 / 65535.0

time: 33.9 us -> 33.9 us (level)
  no operation moved by 1% of the time
where the time goes in v6:
time: 33.9 us; the launch traced here: 33.6 us
  blocking collectives  27.9 us (82%)
  Pallas kernels  5.6 us (17%)
    all_to_all x2, blocking collectives, exchange(): return lax.all_to_all(x, axis, 0, 0, axis_index_groups=[group], tiled=True)  27.9 us
    pallas_call x1, Pallas kernels, local(): pl.pallas_call(pack_kernel, out_shape=(pltpu.VMEM((LEVELS, LANES), jnp.in...  3.85 us
    pallas_call x1, Pallas kernels, local(): pl.pallas_call(radiate_kernel, out_shape=pltpu.VMEM((DISKS, HALF, LANES),...  0.88 us
    pallas_call x1, Pallas kernels, local(): pl.pallas_call(pixel_kernel, out_shape=jax.ShapeDtypeStruct((HOURS * BAND...  0.87 us

profile of v6, /device:TPU:8, one launch (start us, length us, event | category | flops | bytes accessed | tf_op | source)
XLA Modules:
  0.0 33.6 jit_solution(13183032856253273064)
XLA Ops:
  0.0 3.9 %pack.1 = (s32[128,128]{1,0:T(8,128)S(1)}, f32[128,7,8,128]{3,2,1,0:T(8,128)S(1)}, f32[7,8,128]{2,1,0:T(8,128)S(1)}, f32[7,8,128]{2,1,0:T(8,128)S(1)}, f32[8,128...) custom-call(f32[64,128]{1,0:T(8,128)} %bitcast.12, f32[64,128]{1,0:T(8,128)} %bitcast.13, ...), custom_call_target="tpu_custom_call" | custom-call | tf_op jit(solution)/shard_map/pack/pallas_call | solution.py:330
  3.9 21.0 %all_to_all.16 = s32[128,1,128]{2,1,0:T(1,128)S(1)} all-to-all(s32[128,1,128]{2,1,0:T(1,128)S(1)} %bitcast.11), channel_id=1, replica_groups={{300,4,8,12,16,20,24,28,32,36,40,44,48,52,56,60,64,68,72,76,80,84,88,92..., dimensions={0} | all-to-all | bytes 131072 | tf_op jit(solution)/shard_map/all_to_all | solution.py:282
  24.9 0.9 %radiate.1 = bf16[4,8,128]{2,1,0:T(8,128)(2,1)S(1)} custom-call(s32[128,128]{1,0:T(8,128)S(1)} %bitcast.10, f32[128,7,8,128]{3,2,1,0:T(8,128)S(1)} %get-tuple-element.13.gas_ref, f32[7,8,128]{2,1,0:T(8,128)S(1)} %get-tuple-element.14.cloud_ref, f32[7,8,128]{2,1,0:T(8,128)S(1)} %get-tuple-element.15.start_ref, f32[8,128]{1,0:T(8,128)S(1)} %get-tuple-element.16.weight_ref, ...), custom_call_target="tpu_custom_call" | custom-call | tf_op jit(solution)/shard_map/radiate/pallas_call | solution.py:346
  25.8 6.9 %all_to_all.17.rad_ref = bf16[4,8,128]{2,1,0:T(8,128)(2,1)S(1)} all-to-all(bf16[4,8,128]{2,1,0:T(8,128)(2,1)S(1)} %radiate.1), channel_id=1, replica_groups={{2,1,0,3},{6,5,4,7},{10,9,8,11},{14,13,12,15},{18,17,16,19},{22,21,20,2..., dimensions={0} | all-to-all | bytes 16384 | tf_op jit(solution)/shard_map/all_to_all | solution.py:282
  32.7 0.9 %pixels.1 = f32[32,512]{1,0:T(8,128)} custom-call(bf16[4,8,128]{2,1,0:T(8,128)(2,1)S(1)} %all_to_all.17.rad_ref, bf16[256,512]{1,0:T(8,128)(2,1)S(1)} %get-tuple-element.18.mix_ref, s32[4,512]{1,0:T(4,128)} %source_hbm.3, f32[4,512]{1,0:T(4,128)} %factor_hbm.3), custom_call_target="tpu_custom_call" | custom-call | tf_op jit(solution)/shard_map/pixels/pallas_call | solution.py:358

commit v7 on v5

--- a/solution.py
+++ b/solution.py
@@ -33,6 +33,8 @@
 
 
 def swapped_group(size, first):
+    if size == DISKS:
+        return [2, 0, 3, 1]
     return [first if i == 0 else 0 if i == first else i for i in range(size)]
 
 

time: 33.9 us -> 33.9 us (level)
  the two profiles are of different devices: /device:TPU:8 before, /device:TPU:2 now
where the time goes in v7:
time: 33.9 us; the launch traced here: 33.6 us
  blocking collectives  28 us (83%)
  Pallas kernels  5.64 us (17%)
    all_to_all x2, blocking collectives, exchange(): return lax.all_to_all(x, axis, 0, 0, axis_index_groups=[group], tiled=True)  28 us
    pallas_call x1, Pallas kernels, local(): pl.pallas_call(pack_kernel, out_shape=(pltpu.VMEM((LEVELS, LANES), jnp.in...  3.85 us
    pallas_call x1, Pallas kernels, local(): pl.pallas_call(radiate_kernel, out_shape=pltpu.VMEM((DISKS, HALF, LANES),...  0.92 us
    pallas_call x1, Pallas kernels, local(): pl.pallas_call(pixel_kernel, out_shape=jax.ShapeDtypeStruct((HOURS * BAND...  0.87 us

profile of v7, /device:TPU:2, one launch (start us, length us, event | category | flops | bytes accessed | tf_op | source)
XLA Modules:
  0.0 33.6 jit_solution(13833930282292013552)
XLA Ops:
  0.0 3.8 %pack.1 = (s32[128,128]{1,0:T(8,128)S(1)}, f32[128,7,8,128]{3,2,1,0:T(8,128)S(1)}, f32[7,8,128]{2,1,0:T(8,128)S(1)}, f32[7,8,128]{2,1,0:T(8,128)S(1)}, f32[8,128...) custom-call(f32[64,128]{1,0:T(8,128)} %bitcast.12, f32[64,128]{1,0:T(8,128)} %bitcast.13, ...), custom_call_target="tpu_custom_call" | custom-call | tf_op jit(solution)/shard_map/pack/pallas_call | solution.py:332
  3.9 20.0 %all_to_all.16 = s32[128,1,128]{2,1,0:T(1,128)S(1)} all-to-all(s32[128,1,128]{2,1,0:T(1,128)S(1)} %bitcast.11), channel_id=1, replica_groups={{300,4,8,12,16,20,24,28,32,36,40,44,48,52,56,60,64,68,72,76,80,84,88,92..., dimensions={0} | all-to-all | bytes 131072 | tf_op jit(solution)/shard_map/all_to_all | solution.py:284
  23.8 0.9 %radiate.1 = bf16[4,8,128]{2,1,0:T(8,128)(2,1)S(1)} custom-call(s32[128,128]{1,0:T(8,128)S(1)} %bitcast.10, f32[128,7,8,128]{3,2,1,0:T(8,128)S(1)} %get-tuple-element.13.gas_ref, f32[7,8,128]{2,1,0:T(8,128)S(1)} %get-tuple-element.14.cloud_ref, f32[7,8,128]{2,1,0:T(8,128)S(1)} %get-tuple-element.15.start_ref, f32[8,128]{1,0:T(8,128)S(1)} %get-tuple-element.16.weight_ref, ...), custom_call_target="tpu_custom_call" | custom-call | tf_op jit(solution)/shard_map/radiate/pallas_call | solution.py:348
  24.8 8.0 %all_to_all.17.rad_ref = bf16[4,8,128]{2,1,0:T(8,128)(2,1)S(1)} all-to-all(bf16[4,8,128]{2,1,0:T(8,128)(2,1)S(1)} %radiate.1), channel_id=1, replica_groups={{2,0,3,1},{6,4,7,5},{10,8,11,9},{14,12,15,13},{18,16,19,17},{22,20,23,2..., dimensions={0} | all-to-all | bytes 16384 | tf_op jit(solution)/shard_map/all_to_all | solution.py:284
  32.8 0.9 %pixels.1 = f32[32,512]{1,0:T(8,128)} custom-call(bf16[4,8,128]{2,1,0:T(8,128)(2,1)S(1)} %all_to_all.17.rad_ref, bf16[256,512]{1,0:T(8,128)(2,1)S(1)} %get-tuple-element.18.mix_ref, s32[4,512]{1,0:T(4,128)} %source_hbm.3, f32[4,512]{1,0:T(4,128)} %factor_hbm.3), custom_call_target="tpu_custom_call" | custom-call | tf_op jit(solution)/shard_map/pixels/pallas_call | solution.py:360
